TPU v7x, 256 devices: a whole 4x4x8 slice. The times are simulated.
256 devices in a mesh: dom: 8 (over x, core), st: 32 (over y, z).
Axes of the slice: x: 4, y: 4, z: 8, core: 2. Of those that a mesh axis runs over, the one named last changes fastest.
Arguments:
- orbitals: bfloat16 [512, 512, 1024], P('st', 'dom'), may hold values from -6 to 6
- potential: bfloat16 [512, 1024], P('dom'), may hold values from -0.5 to 0.5
- rotation: bfloat16 [512, 512], P('st'), may hold values from -0.25 to 0.25
Outputs:
- rotated: bfloat16 [512, 524288], P(None, ('dom', 'st'))
All inputs are finite; a program needn't handle non-finite values.
Results may differ from a plain program's by a relative error of at most 0.0049.
Values may be sent and summed in bfloat16 or wider, within the bound.
No kernel may reach another device: no remote copies, remote signals or barrier semaphores. Data moves between devices by JAX's collectives and lax.ppermute only.
A program may use at most 64 MiB of HBM per device.

v0:
```python
import jax
import jax.numpy as jnp
from jax import lax
from jax.sharding import PartitionSpec as P

DEGREE = 4
NZ = 32


cheb_shift = 3.75
cheb_scale = 3.25


def extended(block, sides, width):
    for axis, dim in sides:
        count = lax.axis_size(axis)
        forward = [(i, i + 1) for i in range(count - 1)]
        backward = [(target, source) for source, target in forward]
        low = lax.ppermute(
            lax.slice_in_dim(block, block.shape[dim] - width, None, axis=dim), axis, forward
        )
        high = lax.ppermute(lax.slice_in_dim(block, 0, width, axis=dim), axis, backward)
        block = jnp.concatenate([low, block, high], axis=dim)
    return block


def neighbour_sum(center, nz_count):
    row_width = center.shape[2]
    z_position = lax.broadcasted_iota(jnp.int32, (1, 1, row_width), 2) % nz_count
    padded = jnp.pad(center, ((0, 0), (0, 0), (nz_count, nz_count)))
    along_y = padded[:, :, 2 * nz_count :] + padded[:, :, :row_width]
    upper_z = jnp.where(
        z_position < nz_count - 1, padded[:, :, nz_count + 1 : nz_count + 1 + row_width], 0.0
    )
    lower_z = jnp.where(z_position > 0, padded[:, :, nz_count - 1 : nz_count - 1 + row_width], 0.0)
    return along_y + upper_z + lower_z


def hamiltonian(padded_x, local_pot, nz_count):
    center = padded_x[:, 1:-1]
    beside = padded_x[:, 2:] + padded_x[:, :-2] + neighbour_sum(center, nz_count)
    return (3.0 + local_pot) * center - 0.5 * beside


def chebyshev(start, apply_fn, degree):
    previous = start
    current = (apply_fn(start) - cheb_shift * start) / cheb_scale
    for filter_order in range(1, degree):
        following = 2.0 * (apply_fn(current) - cheb_shift * current) / cheb_scale - previous
        previous = current
        current = following
    return current


def local(orbitals, potential, rotation):
    start = orbitals.astype(jnp.float32)
    local_pot = potential.astype(jnp.float32)
    states_dev, planes, row_width = start.shape

    def apply_step(state_field):
        padded = extended(state_field, (("dom", 1),), 1)
        return hamiltonian(padded, local_pot, NZ)

    result = chebyshev(start, apply_step, DEGREE)
    filtered = result.astype(jnp.bfloat16).reshape(states_dev, planes * row_width)
    regrouped = lax.all_to_all(filtered, "st", split_axis=1, concat_axis=0, tiled=True)
    product = jnp.dot(
        lax.all_gather(rotation, "st", axis=0, tiled=True),
        regrouped,
        preferred_element_type=jnp.float32,
    )
    return product.astype(jnp.bfloat16)


def solution(mesh):
    return jax.shard_map(
        local,
        mesh=mesh,
        in_specs=(P("st", "dom", None), P("dom", None), P("st", None)),
        out_specs=P(None, ("dom", "st")),
        check_vma=False,
    )
```

profile of v0, /device:TPU:2, one launch (start us, length us, event | category | flops | bytes accessed | tf_op | source)
XLA Modules:
  0.0 166.8 jit_solution(14921552852424381821)
XLA Ops:
  0.0 1.1 fusion.57
  1.2 1.9 %collective-permute-start = (f32[16,1,1024]{2,1,0:T(1,128)S(1)}, f32[16,1,1024]{2,1,0:T(1,128)S(1)}, u32[]{:S(2)}, u32[]{:S(2)}) collective-permute-start(f32[16,1,1024]{2,1,0:T(1,128)S(1)} %get-tuple-element.13), channel_id=1, source_target_pairs={{32,0},{64,32},{96,64},{128,96},{160,128},{192,160},{224,192},{33,... | collective-permute-start | bytes 196616 | tf_op jit(solution)/shard_map/ppermute | solution.py:22
  3.1 2.4 %collective-permute-start.1 = (f32[16,1,1024]{2,1,0:T(1,128)S(1)}, f32[16,1,1024]{2,1,0:T(1,128)S(1)}, u32[]{:S(2)}, u32[]{:S(2)}) collective-permute-start(f32[16,1,1024]{2,1,0:T(1,128)S(1)} %get-tuple-element.14), channel_id=1, source_target_pairs={{0,32},{32,64},{64,96},{96,128},{128,160},{160,192},{192,224},{1,3... | collective-permute-start | bytes 196616 | tf_op jit(solution)/shard_map/ppermute | solution.py:19
  5.5 2.0 %convert_element_type.21 = f32[16,64,1024]{2,1,0:T(8,128)S(1)} convert(bf16[16,64,1024]{2,1,0:T(8,128)(2,1)} %param.3) | non-fusion elementwise | flops 1048576 | bytes 6291456 | tf_op jit(solution)/shard_map/convert_element_type | solution.py:56
  7.6 0.0 collective-permute-done
  7.6 1.6 collective-permute-done.1
  9.3 4.7 %broadcast_multiply_fusion = (f32[16,64,1024]{2,1,0:T(8,128)S(1)}, f32[16,64,1024]{2,1,0:T(8,128)S(1)}) fusion(f32[16,64,1024]{2,1,0:T(8,128)S(1)} %convert_element_type.21, pred[1024]{0:T(1024)(128)(4,1)S(1)} %get-tuple-element.17, pred[1024]{0:T(1024)(128)(4,1)S(1)} %get-tuple-element.18, f32[16,1,1024]{2,1,0:T(1,128)S(1)} %collective-permute-done.1, ...), kind=kLoop, calls=%fused_computation.73 | loop fusion | flops 15728640 | bytes 12978176 | tf_op jit(solution)/shard_map/div | solution.py:47
  13.9 0.1 fusion.56
  14.0 2.2 %collective-permute-start.2 = (f32[16,1,1024]{2,1,0:T(1,128)S(1)}, f32[16,1,1024]{2,1,0:T(1,128)S(1)}, u32[]{:S(2)}, u32[]{:S(2)}) collective-permute-start(f32[16,1,1024]{2,1,0:T(1,128)S(1)} %get-tuple-element.11), channel_id=1, source_target_pairs={{32,0},{64,32},{96,64},{128,96},{160,128},{192,160},{224,192},{33,... | collective-permute-start | bytes 196616 | tf_op jit(solution)/shard_map/ppermute | solution.py:22
  16.2 2.2 %collective-permute-start.3 = (f32[16,1,1024]{2,1,0:T(1,128)S(1)}, f32[16,1,1024]{2,1,0:T(1,128)S(1)}, u32[]{:S(2)}, u32[]{:S(2)}) collective-permute-start(f32[16,1,1024]{2,1,0:T(1,128)S(1)} %get-tuple-element.12), channel_id=1, source_target_pairs={{0,32},{32,64},{64,96},{96,128},{128,160},{160,192},{192,224},{1,3... | collective-permute-start | bytes 196616 | tf_op jit(solution)/shard_map/ppermute | solution.py:19
  18.4 0.0 collective-permute-done.2
  18.4 3.4 %collective-permute-done.3 = f32[16,1,1024]{2,1,0:T(1,128)S(1)} collective-permute-done((f32[16,1,1024]{2,1,0:T(1,128)S(1)}, f32[16,1,1024]{2,1,0:T(1,128)S(1)}, u32[]{:S(2)}, u32[]{:S(2)}) %collective-permute-start.3) | collective-permute-done | bytes 65568 | tf_op jit(solution)/shard_map/ppermute | solution.py:19
  21.8 6.1 %fusion.17 = f32[16,64,1024]{2,1,0:T(8,128)S(1)} fusion(f32[16,64,1024]{2,1,0:T(8,128)S(1)} %get-tuple-element.5, f32[16,1,1024]{2,1,0:T(1,128)S(1)} %collective-permute-done.3, f32[16,1,1024]{2,1,0:T(1,128)S(1)} %collective-permute-done.2, f32[16,64,1024]{2,1,0:T(8,128)S(1)} %get-tuple-element.6, f32[64,1024]{1,0:T(8,128)S(1)} %get-tuple-element.15, ...), kind=kLoop, calls=%fused_computation.33 | loop fusion | flops 17825792 | bytes 15075328 | tf_op jit(solution)/shard_map/sub | solution.py:49
  27.9 0.1 fusion.55
  28.0 1.9 %collective-permute-start.4 = (f32[16,1,1024]{2,1,0:T(1,128)S(1)}, f32[16,1,1024]{2,1,0:T(1,128)S(1)}, u32[]{:S(2)}, u32[]{:S(2)}) collective-permute-start(f32[16,1,1024]{2,1,0:T(1,128)S(1)} %get-tuple-element.9), channel_id=1, source_target_pairs={{32,0},{64,32},{96,64},{128,96},{160,128},{192,160},{224,192},{33,... | collective-permute-start | bytes 196616 | tf_op jit(solution)/shard_map/ppermute | solution.py:22
  30.0 2.4 %collective-permute-start.5 = (f32[16,1,1024]{2,1,0:T(1,128)S(1)}, f32[16,1,1024]{2,1,0:T(1,128)S(1)}, u32[]{:S(2)}, u32[]{:S(2)}) collective-permute-start(f32[16,1,1024]{2,1,0:T(1,128)S(1)} %get-tuple-element.10), channel_id=1, source_target_pairs={{0,32},{32,64},{64,96},{96,128},{128,160},{160,192},{192,224},{1,3... | collective-permute-start | bytes 196616 | tf_op jit(solution)/shard_map/ppermute | solution.py:19
  32.4 0.0 collective-permute-done.4
  32.4 3.2 %collective-permute-done.5 = f32[16,1,1024]{2,1,0:T(1,128)S(1)} collective-permute-done((f32[16,1,1024]{2,1,0:T(1,128)S(1)}, f32[16,1,1024]{2,1,0:T(1,128)S(1)}, u32[]{:S(2)}, u32[]{:S(2)}) %collective-permute-start.5) | collective-permute-done | bytes 65568 | tf_op jit(solution)/shard_map/ppermute | solution.py:19
  35.6 4.7 %fusion.28 = f32[16,64,1024]{2,1,0:T(8,128)S(1)} fusion(f32[16,64,1024]{2,1,0:T(8,128)S(1)} %fusion.17, f32[16,1,1024]{2,1,0:T(1,128)S(1)} %collective-permute-done.5, f32[16,1,1024]{2,1,0:T(1,128)S(1)} %collective-permute-done.4, f32[16,64,1024]{2,1,0:T(8,128)S(1)} %get-tuple-element.6, f32[64,1024]{1,0:T(8,128)S(1)} %get-tuple-element.16, ...), kind=kLoop, calls=%fused_computation.44 | loop fusion | flops 17825792 | bytes 12978176 | tf_op jit(solution)/shard_map/sub | solution.py:49
  40.3 0.1 fusion.54
  40.4 1.9 %collective-permute-start.6 = (f32[16,1,1024]{2,1,0:T(1,128)S(1)}, f32[16,1,1024]{2,1,0:T(1,128)S(1)}, u32[]{:S(2)}, u32[]{:S(2)}) collective-permute-start(f32[16,1,1024]{2,1,0:T(1,128)S(1)} %get-tuple-element.7), channel_id=1, source_target_pairs={{32,0},{64,32},{96,64},{128,96},{160,128},{192,160},{224,192},{33,... | collective-permute-start | bytes 196616 | tf_op jit(solution)/shard_map/ppermute | solution.py:22
  42.3 2.6 %collective-permute-start.7 = (f32[16,1,1024]{2,1,0:T(1,128)S(1)}, f32[16,1,1024]{2,1,0:T(1,128)S(1)}, u32[]{:S(2)}, u32[]{:S(2)}) collective-permute-start(f32[16,1,1024]{2,1,0:T(1,128)S(1)} %get-tuple-element.8), channel_id=1, source_target_pairs={{0,32},{32,64},{64,96},{96,128},{128,160},{160,192},{192,224},{1,3... | collective-permute-start | bytes 196616 | tf_op jit(solution)/shard_map/ppermute | solution.py:19
  44.9 0.0 collective-permute-done.6
  44.9 3.0 %collective-permute-done.7 = f32[16,1,1024]{2,1,0:T(1,128)S(1)} collective-permute-done((f32[16,1,1024]{2,1,0:T(1,128)S(1)}, f32[16,1,1024]{2,1,0:T(1,128)S(1)}, u32[]{:S(2)}, u32[]{:S(2)}) %collective-permute-start.7) | collective-permute-done | bytes 65568 | tf_op jit(solution)/shard_map/ppermute | solution.py:19
  47.9 5.8 %fusion.40 = bf16[16,64,1024]{2,1,0:T(8,128)(2,1)} fusion(f32[16,64,1024]{2,1,0:T(8,128)S(1)} %fusion.17, f32[16,64,1024]{2,1,0:T(8,128)S(1)} %fusion.28, f32[16,1,1024]{2,1,0:T(1,128)S(1)} %collective-permute-done.7, f32[16,1,1024]{2,1,0:T(1,128)S(1)} %collective-permute-done.6, f32[64,1024]{1,0:T(8,128)S(1)} %get-tuple-element.16, ...), kind=kLoop, calls=%fused_computation.56 | loop fusion | flops 17825792 | bytes 10881024 | tf_op jit(solution)/shard_map/convert_element_type | solution.py:65
  53.7 2.7 %all_to_all.14 = bf16[16,32,2048]{2,1,0:T(8,128)(2,1)S(1)} reshape(bf16[16,64,1024]{2,1,0:T(8,128)(2,1)} %fusion.40) | data formatting | bytes 4194304 | tf_op jit(solution)/shard_map/all_to_all | solution.py:66
  56.3 0.0 copy-start.1
  56.4 2.5 %copy.8 = bf16[16,32,2048]{2,0,1:T(8,128)(2,1)} copy(bf16[16,32,2048]{2,1,0:T(8,128)(2,1)S(1)} %all_to_all.14) | data formatting | bytes 4194304 | tf_op jit(solution)/shard_map/all_to_all | solution.py:66
  58.8 10.9 %all-to-all-start = ((bf16[16,32,2048]{2,0,1:T(8,128)(2,1)}), bf16[16,32,2048]{2,0,1:T(8,128)(2,1)S(1)}, u32[]{:S(2)}, u32[]{:S(2)}) async-start(bf16[16,32,2048]{2,0,1:T(8,128)(2,1)} %copy.8), calls=%async_computation | async-start | bytes 4194304 | tf_op jit(solution)/shard_map/all_to_all | solution.py:66
  69.7 90.6 %all_gather.3 = bf16[512,512]{1,0:T(8,128)(2,1)S(1)} all-gather(bf16[16,512]{1,0:T(8,128)(2,1)S(1)} %copy-done.1), channel_id=1, replica_groups=mesh['dom'=8,'st'=32] {'st'}, dimensions={0}, use_global_device_ids=true | all-gather | bytes 540672 | tf_op jit(solution)/shard_map/all_gather | solution.py:68
  160.3 2.7 %fusion.47 = bf16[512,2048]{0,1:T(8,128)(2,1)} fusion(bf16[512,2048]{1,0:T(8,128)(2,1)S(1)} %bitcast.7, bf16[512,512]{1,0:T(8,128)(2,1)S(1)} %all_gather.3), kind=kOutput, calls=%fused_computation.72 | convolution fusion | flops 1074790400 | bytes 4718592 | tf_op jit(solution)/shard_map/dot_general | solution.py:67
  162.9 3.9 %copy.9 = bf16[512,2048]{1,0:T(8,128)(2,1)} copy(bf16[512,2048]{0,1:T(8,128)(2,1)} %fusion.47) | data formatting | bytes 4194304 | tf_op jit(solution)/shard_map/convert_element_type | solution.py:72
  (6 shorter events, 0.1 us)
Async XLA Ops:
  0.0 7.6 %copy-start = (bf16[64,1024]{1,0:T(8,128)(2,1)S(1)}, bf16[64,1024]{1,0:T(8,128)(2,1)}, u32[]{:S(2)}) copy-start(bf16[64,1024]{1,0:T(8,128)(2,1)} %param.4) | copy-start | bytes 393220
  1.2 6.5 %collective-permute-start = (f32[16,1,1024]{2,1,0:T(1,128)S(1)}, f32[16,1,1024]{2,1,0:T(1,128)S(1)}, u32[]{:S(2)}, u32[]{:S(2)}) collective-permute-start(f32[16,1,1024]{2,1,0:T(1,128)S(1)} %get-tuple-element.13), channel_id=1, source_target_pairs={{32,0},{64,32},{96,64},{128,96},{160,128},{192,160},{224,192},{33,... | collective-permute-start | bytes 196616 | tf_op jit(solution)/shard_map/ppermute | solution.py:22
  3.1 6.2 %collective-permute-start.1 = (f32[16,1,1024]{2,1,0:T(1,128)S(1)}, f32[16,1,1024]{2,1,0:T(1,128)S(1)}, u32[]{:S(2)}, u32[]{:S(2)}) collective-permute-start(f32[16,1,1024]{2,1,0:T(1,128)S(1)} %get-tuple-element.14), channel_id=1, source_target_pairs={{0,32},{32,64},{64,96},{96,128},{128,160},{160,192},{192,224},{1,3... | collective-permute-start | bytes 196616 | tf_op jit(solution)/shard_map/ppermute | solution.py:19
  14.0 4.3 %collective-permute-start.2 = (f32[16,1,1024]{2,1,0:T(1,128)S(1)}, f32[16,1,1024]{2,1,0:T(1,128)S(1)}, u32[]{:S(2)}, u32[]{:S(2)}) collective-permute-start(f32[16,1,1024]{2,1,0:T(1,128)S(1)} %get-tuple-element.11), channel_id=1, source_target_pairs={{32,0},{64,32},{96,64},{128,96},{160,128},{192,160},{224,192},{33,... | collective-permute-start | bytes 196616 | tf_op jit(solution)/shard_map/ppermute | solution.py:22
  16.2 5.6 %collective-permute-start.3 = (f32[16,1,1024]{2,1,0:T(1,128)S(1)}, f32[16,1,1024]{2,1,0:T(1,128)S(1)}, u32[]{:S(2)}, u32[]{:S(2)}) collective-permute-start(f32[16,1,1024]{2,1,0:T(1,128)S(1)} %get-tuple-element.12), channel_id=1, source_target_pairs={{0,32},{32,64},{64,96},{96,128},{128,160},{160,192},{192,224},{1,3... | collective-permute-start | bytes 196616 | tf_op jit(solution)/shard_map/ppermute | solution.py:19
  28.0 4.3 %collective-permute-start.4 = (f32[16,1,1024]{2,1,0:T(1,128)S(1)}, f32[16,1,1024]{2,1,0:T(1,128)S(1)}, u32[]{:S(2)}, u32[]{:S(2)}) collective-permute-start(f32[16,1,1024]{2,1,0:T(1,128)S(1)} %get-tuple-element.9), channel_id=1, source_target_pairs={{32,0},{64,32},{96,64},{128,96},{160,128},{192,160},{224,192},{33,... | collective-permute-start | bytes 196616 | tf_op jit(solution)/shard_map/ppermute | solution.py:22
  30.0 5.6 %collective-permute-start.5 = (f32[16,1,1024]{2,1,0:T(1,128)S(1)}, f32[16,1,1024]{2,1,0:T(1,128)S(1)}, u32[]{:S(2)}, u32[]{:S(2)}) collective-permute-start(f32[16,1,1024]{2,1,0:T(1,128)S(1)} %get-tuple-element.10), channel_id=1, source_target_pairs={{0,32},{32,64},{64,96},{96,128},{128,160},{160,192},{192,224},{1,3... | collective-permute-start | bytes 196616 | tf_op jit(solution)/shard_map/ppermute | solution.py:19
  40.4 4.5 %collective-permute-start.6 = (f32[16,1,1024]{2,1,0:T(1,128)S(1)}, f32[16,1,1024]{2,1,0:T(1,128)S(1)}, u32[]{:S(2)}, u32[]{:S(2)}) collective-permute-start(f32[16,1,1024]{2,1,0:T(1,128)S(1)} %get-tuple-element.7), channel_id=1, source_target_pairs={{32,0},{64,32},{96,64},{128,96},{160,128},{192,160},{224,192},{33,... | collective-permute-start | bytes 196616 | tf_op jit(solution)/shard_map/ppermute | solution.py:22
  42.3 5.6 %collective-permute-start.7 = (f32[16,1,1024]{2,1,0:T(1,128)S(1)}, f32[16,1,1024]{2,1,0:T(1,128)S(1)}, u32[]{:S(2)}, u32[]{:S(2)}) collective-permute-start(f32[16,1,1024]{2,1,0:T(1,128)S(1)} %get-tuple-element.8), channel_id=1, source_target_pairs={{0,32},{32,64},{64,96},{96,128},{128,160},{160,192},{192,224},{1,3... | collective-permute-start | bytes 196616 | tf_op jit(solution)/shard_map/ppermute | solution.py:19
  56.3 13.4 %copy-start.1 = (bf16[16,512]{1,0:T(8,128)(2,1)S(1)}, bf16[16,512]{1,0:T(8,128)(2,1)}, u32[]{:S(2)}) copy-start(bf16[16,512]{1,0:T(8,128)(2,1)} %param.5) | copy-start | bytes 49156
  58.8 101.5 %all-to-all-start = ((bf16[16,32,2048]{2,0,1:T(8,128)(2,1)}), bf16[16,32,2048]{2,0,1:T(8,128)(2,1)S(1)}, u32[]{:S(2)}, u32[]{:S(2)}) async-start(bf16[16,32,2048]{2,0,1:T(8,128)(2,1)} %copy.8), calls=%async_computation | async-start | bytes 4194304 | tf_op jit(solution)/shard_map/all_to_all | solution.py:66
where the time goes:
time: 167 us
  blocking collectives  90.6 us (54%)
  starting transfers between devices  28.4 us (17%)
  other arithmetic  23.4 us (14%)
  waiting for transfers between devices  11.2 us (7%)
  local copies, waits for them, and re-layouts  10.5 us (6%)
  matrix products  2.65 us (2%)
    all_gather x1, blocking collectives, local(): lax.all_gather(rotation, 'st', axis=0, tiled=True)  90.6 us
    ppermute x4, waiting for transfers between devices, extended(): lax.ppermute(lax.slice_in_dim(block, block.shape[dim] - width, None, axis...  11.2 us
    all_to_all x1, starting transfers between devices, local(): lax.all_to_all(filtered, 'st', split_axis=1, concat_axis=0, tiled=True)  10.9 us
    sub x2, other arithmetic, chebyshev(): 2.0 * (apply_fn(current) - cheb_shift * current) / cheb_scale - previous  10.8 us
    ppermute x4, starting transfers between devices, extended(): lax.ppermute(lax.slice_in_dim(block, block.shape[dim] - width, None, axis...  9.57 us
    ppermute x4, starting transfers between devices, extended(): lax.ppermute(lax.slice_in_dim(block, 0, width, axis=dim), axis, backward)  7.92 us
    convert_element_type x1, other arithmetic, local(): result.astype(jnp.bfloat16).reshape(states_dev, planes * row_width)  5.77 us
    all_to_all x2, local copies, waits for them, and re-layouts, local(): lax.all_to_all(filtered, 'st', split_axis=1, concat_axis=0, tiled=True)  5.14 us
  transfers between devices with their start and end apart: 9, of which 4 were waited for; matrix products, arithmetic and copies ran while one was open for 1% of the time, Pallas kernels for 0%

commit v1 on v0

v1 whole, which is shorter than its diff:
```python
import functools

import jax
import jax.numpy as jnp
from jax import lax
from jax.experimental import pallas as pl
from jax.experimental.pallas import tpu as pltpu
from jax.sharding import PartitionSpec as P

DEGREE = 4
NZ = 32
LANES = 128

cheb_shift = 3.75
cheb_scale = 3.25

F32 = jnp.float32
BF16 = jnp.bfloat16

INNER_Y = LANES // NZ
RUN = NZ + 8
PLANE = INNER_Y * RUN


def one_hot(rows, cols, want):
    r = lax.broadcasted_iota(jnp.int32, (rows, cols), 0)
    c = lax.broadcasted_iota(jnp.int32, (rows, cols), 1)
    return jnp.where(c == want(r), 1.0, 0.0).astype(BF16)


def turned(block):
    eye = one_hot(LANES, LANES, lambda r: r)
    return lax.dot_general(eye, block, (((1,), (1,)), ((), ())), preferred_element_type=F32)


def stacked(rows, states, first, count):
    width = rows.shape[1]
    return jnp.concatenate(
        [
            rows[(first + p) * states : (first + p + 1) * states, j * LANES : (j + 1) * LANES]
            for p in range(count)
            for j in range(width // LANES)
        ],
        axis=0,
    )


def edges_kernel(first_ref, last_ref, pot_first_ref, pot_last_ref, low_ref, high_ref):
    states, slab, width = first_ref.shape
    rows = DEGREE * states
    pick = one_hot(rows, states * slab, lambda r: (r % states) * slab + r // states)
    first = first_ref[...].reshape(states * slab, width)
    low_ref[:rows] = jnp.dot(pick, first, preferred_element_type=F32).astype(BF16)
    low_ref[rows:] = pot_first_ref[...]
    pick = one_hot(
        rows, states * slab, lambda r: (r % states) * slab + r // states + (slab - DEGREE)
    )
    last = last_ref[...].reshape(states * slab, width)
    high_ref[:rows] = jnp.dot(pick, last, preferred_element_type=F32).astype(BF16)
    high_ref[rows:] = pot_last_ref[...]


def edges(orbitals, potential):
    states, planes, width = orbitals.shape
    slab = 8
    last = planes // slab - 1
    out = jax.ShapeDtypeStruct((DEGREE * states + slab, width), BF16)
    return pl.pallas_call(
        edges_kernel,
        grid=(1,),
        in_specs=[
            pl.BlockSpec((states, slab, width), lambda i: (0, 0, 0)),
            pl.BlockSpec((states, slab, width), lambda i: (0, last, 0)),
            pl.BlockSpec((slab, width), lambda i: (0, 0)),
            pl.BlockSpec((slab, width), lambda i: (last, 0)),
        ],
        out_specs=[pl.BlockSpec(out.shape, lambda i: (0, 0))] * 2,
        out_shape=[out, out],
        name="edges",
    )(orbitals, orbitals, potential, potential)


def spread(pot_rows, states):
    count = pot_rows.shape[0]
    repeat = one_hot(count * states, count, lambda r: r // states)
    return jnp.dot(repeat, pot_rows, preferred_element_type=F32).astype(BF16)


def prepare_kernel(x_ref, pot_ref, field_ref, pot_out_ref):
    states, group, width = x_ref.shape
    pick = one_hot(
        states * group, states * group, lambda r: (r % states) * group + r // states
    )
    rows = x_ref[...].reshape(states * group, width)
    rows = jnp.dot(pick, rows, preferred_element_type=F32).astype(BF16)
    pot = spread(pot_ref[...], states)
    for p in range(0, group, 2):
        for source, target in ((rows, field_ref), (pot, pot_out_ref)):
            both = turned(stacked(source, states, p, 2)).astype(BF16)
            target[p] = both[:, :LANES]
            target[p + 1] = both[:, LANES:]


def prepare(orbitals, potential):
    states, planes, width = orbitals.shape
    group = 16
    out = jax.ShapeDtypeStruct((planes, LANES, LANES), BF16)
    return pl.pallas_call(
        prepare_kernel,
        grid=(planes // group,),
        in_specs=[
            pl.BlockSpec((states, group, width), lambda i: (0, i, 0)),
            pl.BlockSpec((group, width), lambda i: (i, 0)),
        ],
        out_specs=[pl.BlockSpec((group, LANES, LANES), lambda i: (i, 0, 0))] * 2,
        out_shape=[out, out],
        cost_estimate=pl.CostEstimate(
            flops=4 * 2 * states * planes * width * 256, transcendentals=0, bytes_accessed=8 << 20
        ),
        name="prepare",
    )(orbitals, potential)


def filter_kernel(
    edge_ref, field_hbm, pot_hbm, low_ref, high_ref, out_hbm,
    even, odd, coef, field_ref, pot_ref, done_ref, out_ref, in_sems, out_sems,
):
    planes = field_ref.shape[0]
    owners, states, points = out_ref.shape
    width = LANES * (LANES // states)
    halo = DEGREE
    b = 1.0 / cheb_scale
    runs = [(r, q) for r in range(INNER_Y) for q in range(NZ // 8)]

    loads = [
        pltpu.make_async_copy(field_hbm, field_ref, in_sems.at[0]),
        pltpu.make_async_copy(pot_hbm, pot_ref, in_sems.at[1]),
    ]
    for load in loads:
        load.start()

    def scaled(p):
        return (p - (cheb_shift - 3.0)) * 2.0

    def put(buffer, plane, values):
        for r in range(INNER_Y):
            at = pl.multiple_of(plane * PLANE + r * RUN + 8, 8)
            buffer[pl.ds(at, NZ), :] = values[r * NZ : (r + 1) * NZ]

    zero = jnp.zeros((8, LANES), F32)

    def clear(i, carry):
        for p in range(4):
            for r in range(INNER_Y):
                at = pl.multiple_of((i * 4 + p) * PLANE + r * RUN, 8)
                even[pl.ds(at, 8), :] = zero
                odd[pl.ds(at, 8), :] = zero
        return carry

    lax.fori_loop(0, (planes + 2 * halo) // 4, clear, 0)
    even[(planes + 2 * halo) * PLANE :, :] = zero
    odd[(planes + 2 * halo) * PLANE :, :] = zero

    rows = DEGREE * states
    for ref, base, at in ((low_ref, 0, 4), (high_ref, halo + planes, 0)):
        field = ref[:rows]
        pot = spread(ref[rows:], states)
        for p in range(0, halo, 2):
            both = turned(stacked(field, states, p, 2))
            put(even, base + p, both[:, :LANES])
            put(even, base + p + 1, both[:, LANES:])
            both = scaled(turned(stacked(pot, states, at + p, 2)))
            coef[base + p] = both[:, :LANES]
            coef[base + p + 1] = both[:, LANES:]

    for load in loads:
        load.wait()

    def fill(i, carry):
        for r in range(2):
            p = i * 2 + r
            put(even, halo + p, field_ref[p].astype(F32))
            coef[halo + p] = scaled(pot_ref[p].astype(F32))
        return carry

    lax.fori_loop(0, planes // 2, fill, 0)

    lane = lax.broadcasted_iota(jnp.int32, (8, LANES), 1)
    first_y = lane < states
    last_y = lane >= LANES - states

    def step(k, plane):
        src, dst = (even, odd) if k % 2 == 1 else (odd, even)
        base = pl.multiple_of(plane * PLANE, 8)

        def rows_at(offset, r, q):
            return src[pl.ds(base + (offset + r * RUN + 8 + q * 8), 8), :]

        here = {rq: rows_at(0, *rq) for rq in runs}
        results = {}
        for r, q in runs:
            v = here[r, q]
            if r > 0:
                below = here[r - 1, q]
            else:
                below = jnp.where(first_y, 0.0, pltpu.roll(here[INNER_Y - 1, q], states, 1))
            if r < INNER_Y - 1:
                above = here[r + 1, q]
            else:
                above = jnp.where(last_y, 0.0, pltpu.roll(here[0, q], LANES - states, 1))
            along_z = rows_at(-1, r, q) + rows_at(1, r, q)
            along_x = rows_at(-PLANE, r, q) + rows_at(PLANE, r, q)
            a = coef[plane, r * NZ + q * 8 : r * NZ + q * 8 + 8, :]
            t = a * v - ((below + above) + (along_z + along_x))
            if k == 1:
                results[r, q] = (0.5 * b) * t
            else:
                results[r, q] = b * t - dst[pl.ds(base + (r * RUN + 8 + q * 8), 8), :]
        return results

    def store(k, plane, results):
        dst = odd if k % 2 == 1 else even
        base = pl.multiple_of(plane * PLANE, 8)
        for r, q in runs:
            dst[pl.ds(base + (r * RUN + 8 + q * 8), 8), :] = results[r, q]

    unroll = 4
    for k in range(1, DEGREE):
        def outer(side, plane, carry, k=k):
            flag = edge_ref[side]
            store(k, plane, {rq: v * flag for rq, v in step(k, plane).items()})
            return carry

        lax.fori_loop(k, halo, functools.partial(outer, 0), 0)
        lax.fori_loop(halo + planes, 2 * halo + planes - k, functools.partial(outer, 1), 0)

        def body(i, carry, k=k):
            results = [step(k, halo + unroll * i + r) for r in range(unroll)]
            for r in range(unroll):
                store(k, halo + unroll * i + r, results[r])
            return carry

        lax.fori_loop(0, planes // unroll, body, 0)

    per = points // width
    batch = unroll // per

    def send(i):
        return pltpu.make_async_copy(
            out_ref.at[pl.ds(i * batch, batch)], out_hbm.at[pl.ds(i * batch, batch)], out_sems.at[i]
        )

    def finish(i):
        for n in range(batch):
            at = pl.multiple_of((i * batch + n) * per * LANES, per * LANES)
            out = turned(done_ref[pl.ds(at, per * LANES), :]).astype(BF16)
            for r in range(per):
                for j in range(width // LANES):
                    out_ref[
                        i * batch + n, :, r * width + j * LANES : r * width + (j + 1) * LANES
                    ] = out[j * states : (j + 1) * states, r * LANES : (r + 1) * LANES]

    def last(i):
        for r in range(unroll):
            res = step(DEGREE, halo + unroll * i + r)
            values = jnp.concatenate([res[rq].astype(BF16) for rq in runs], axis=0)
            at = pl.multiple_of((unroll * i + r) * LANES, LANES)
            done_ref[pl.ds(at, LANES), :] = values

    def both(i, carry):
        finish(i - 1)
        last(i)
        send(i - 1).start()
        return carry

    count = planes // unroll
    last(0)
    lax.fori_loop(1, count, both, 0)
    finish(count - 1)
    send(count - 1).start()
    for i in range(count):
        send(i).wait()


def chebyshev(field, pot, low, high, edge, owners, states):
    planes = field.shape[0]
    points = planes * LANES * LANES // states // owners
    total = planes + 2 * DEGREE
    vmem = pl.BlockSpec(memory_space=pltpu.VMEM)
    anywhere = pl.BlockSpec(memory_space=pl.ANY)
    return pl.pallas_call(
        filter_kernel,
        in_specs=[pl.BlockSpec(memory_space=pltpu.SMEM), anywhere, anywhere, vmem, vmem],
        out_specs=anywhere,
        out_shape=jax.ShapeDtypeStruct((owners, states, points), BF16),
        scratch_shapes=[
            pltpu.VMEM((total * PLANE + 8, LANES), F32),
            pltpu.VMEM((total * PLANE + 8, LANES), F32),
            pltpu.VMEM((total, LANES, LANES), F32),
            pltpu.VMEM(field.shape, BF16),
            pltpu.VMEM(pot.shape, BF16),
            pltpu.VMEM((planes * LANES, LANES), BF16),
            pltpu.VMEM((owners, states, points), BF16),
            pltpu.SemaphoreType.DMA((2,)),
            pltpu.SemaphoreType.DMA((planes // 4,)),
        ],
        name="chebyshev",
    )(edge, field, pot, low, high)


def rotate_kernel(r_ref, f_ref, out_ref):
    out_ref[...] = jnp.dot(r_ref[...], f_ref[...], preferred_element_type=F32).astype(BF16)


def rotate(rotation, filtered):
    total, points = filtered.shape
    tile = 512
    return pl.pallas_call(
        rotate_kernel,
        grid=(points // tile,),
        in_specs=[
            pl.BlockSpec(rotation.shape, lambda i: (0, 0)),
            pl.BlockSpec((total, tile), lambda i: (0, i)),
        ],
        out_specs=pl.BlockSpec((rotation.shape[0], tile), lambda i: (0, i)),
        out_shape=jax.ShapeDtypeStruct((rotation.shape[0], points), BF16),
        name="rotate",
    )(rotation, filtered)


def order_kernel(place_ref, *refs):
    *parts, out_ref = refs
    dom, y, z = place_ref[0], place_ref[1], place_ref[2]
    doms, ys = place_ref[3], place_ref[4]
    total, cols = out_ref.shape
    own = parts[0].shape[0]
    r = lax.broadcasted_iota(jnp.int32, (8, total), 1) // own

    def bit(n):
        return (r >> n) & 1

    source = ((dom + 2 * doms - 4 * bit(2) - 2 * bit(1)) & (doms - 1)) ^ bit(0)
    zs = (z + doms - source) & (doms - 1)
    y_source = (y + 2 * ys - bit(3) - 2 * bit(4)) & (ys - 1)
    want = (y_source * doms + zs) * own
    want = want + lax.broadcasted_iota(jnp.int32, (8, total), 1) % own
    rows = lax.broadcasted_iota(jnp.int32, (total, total), 0)
    pick = jnp.where(rows == jnp.broadcast_to(want[:1], (total, total)), 1.0, 0.0).astype(BF16)
    gathered = jnp.concatenate([p[...] for p in parts], axis=0)
    out_ref[...] = jnp.dot(pick, gathered, preferred_element_type=F32).astype(BF16)


def ordered(place, parts, total):
    vmem = pl.BlockSpec(memory_space=pltpu.VMEM)
    cols = parts[0].shape[1]
    return pl.pallas_call(
        order_kernel,
        in_specs=[pl.BlockSpec(memory_space=pltpu.SMEM)] + [vmem] * len(parts),
        out_specs=vmem,
        out_shape=jax.ShapeDtypeStruct((total, cols), BF16),
        name="order",
    )(place, *parts)


def local(sizes, orbitals, potential, rotation):
    doms, owners = sizes
    zs = doms
    ys = owners // zs
    states = orbitals.shape[0]
    me, spot = lax.axis_index("dom"), lax.axis_index("st")
    up = [(i, i + 1) for i in range(doms - 1)]
    down = [(i + 1, i) for i in range(doms - 1)]
    low_send, high_send = edges(orbitals, potential)
    low = lax.ppermute(high_send, "dom", up)
    high = lax.ppermute(low_send, "dom", down)
    shift = [
        (d * owners + y * zs + z, d * owners + y * zs + (z + d) % zs)
        for d in range(doms)
        for y in range(ys)
        for z in range(zs)
    ]
    rows = lax.ppermute(rotation, ("dom", "st"), shift)
    field, pot = prepare(orbitals, potential)
    rows, field = lax.optimization_barrier((rows, field))
    edge = jnp.stack([me > 0, me < doms - 1]).astype(F32)
    filtered = chebyshev(field, pot, low, high, edge, owners, states)
    rows, _ = lax.optimization_barrier((rows, filtered))
    regrouped = lax.all_to_all(filtered, "st", split_axis=0, concat_axis=0, tiled=True)
    parts = [rows]
    swap = [(i, i ^ 1) for i in range(doms)]
    for perm, axis in (
        (swap, "dom"),
        ([(i, (i + 2) % doms) for i in range(doms)], "dom"),
        ([(i, (i + 4) % doms) for i in range(doms)], "dom"),
        ([(i, (i + zs) % owners) for i in range(owners)], "st"),
        ([(i, (i + 2 * zs) % owners) for i in range(owners)], "st"),
    ):
        parts.append(lax.ppermute(parts[0] if len(parts) == 1 else jnp.concatenate(parts), axis, perm))
    place = jnp.stack([me, spot // zs, spot % zs, jnp.int32(doms), jnp.int32(ys)])
    total = owners * states
    matrix = ordered(place, parts, total)
    return rotate(matrix, regrouped.reshape(total, regrouped.shape[2]))


def solution(mesh):
    sizes = (mesh.shape["dom"], mesh.shape["st"])
    return jax.shard_map(
        functools.partial(local, sizes),
        mesh=mesh,
        in_specs=(P("st", "dom", None), P("dom", None), P("st", None)),
        out_specs=P(None, ("dom", "st")),
        check_vma=False,
    )
```

time: 167 us -> 103 us (0.62)
  blocking collectives: 90.6 us -> 0 us
  Pallas kernels: 0 us -> 30.9 us
  waiting for transfers between devices: 11.2 us -> 40.3 us
  other arithmetic: 23.4 us -> 0.68 us
  local copies, waits for them, and re-layouts: 10.5 us -> 3.35 us
  matrix products: 2.65 us -> 0 us
    all_gather x1 -> x0, blocking collectives: 90.6 us -> none  [local(): lax.all_gather(rotation, 'st', axis=0, tiled=True)]
    pallas_call x0 -> x5, Pallas kernels: none -> 30.9 us  [the longest x1 16.1 us: chebyshev(): pl.pallas_call(filter_kernel, in_specs=[pl.BlockSpec(memory_space=pltpu.S...]
    ppermute x8, waiting for transfers between devices: 11.2 us -> 26.9 us  [the longest x5 26.9 us: local(): lax.ppermute(parts[0] if len(parts) == 1 else jnp.concatenate(parts), axi...]
    all_to_all x1, waiting for transfers between devices: 0.01 us -> 13.4 us  [local(): lax.all_to_all(filtered, 'st', split_axis=0, concat_axis=0, tiled=True)]
    sub x2 -> x0, other arithmetic: 10.8 us -> none  [chebyshev(): 2.0 * (apply_fn(current) - cheb_shift * current) / cheb_scale - previous]
    convert_element_type x2 -> x1, other arithmetic: 7.82 us -> 0.66 us  [local(): edge = jnp.stack([me > 0, me < doms - 1]).astype(F32)]
    all_to_all x2 -> x0, local copies, waits for them, and re-layouts: 5.14 us -> none  [local(): lax.all_to_all(filtered, 'st', split_axis=1, concat_axis=0, tiled=True)]
    div x1 -> x0, other arithmetic: 4.65 us -> none  [chebyshev(): current = (apply_fn(start) - cheb_shift * start) / cheb_scale]
  transfers between devices with their start and end apart: 9 -> 9, of which waited for: 4 -> 6; matrix products, arithmetic and copies ran while one was open for 1% -> 1% of each run, Pallas kernels for 0% -> 10%
where the time goes in v1:
time: 103 us; the launch traced here: 102 us
  waiting for transfers between devices  40.3 us (39%)
  Pallas kernels  30.9 us (30%)
  starting transfers between devices  27 us (26%)
  local copies, waits for them, and re-layouts  3.35 us (3%)
    ppermute x5, waiting for transfers between devices, local(): lax.ppermute(parts[0] if len(parts) == 1 else jnp.concatenate(parts), axi...  26.9 us
    pallas_call x1, Pallas kernels, chebyshev(): pl.pallas_call(filter_kernel, in_specs=[pl.BlockSpec(memory_space=pltpu.S...  16.1 us
    all_to_all x1, waiting for transfers between devices, local(): lax.all_to_all(filtered, 'st', split_axis=0, concat_axis=0, tiled=True)  13.4 us
    all_to_all x1, starting transfers between devices, local(): lax.all_to_all(filtered, 'st', split_axis=0, concat_axis=0, tiled=True)  9.69 us
    ppermute x5, starting transfers between devices, local(): lax.ppermute(parts[0] if len(parts) == 1 else jnp.concatenate(parts), axi...  6.56 us
    pallas_call x1, Pallas kernels, prepare(): pl.pallas_call(prepare_kernel, grid=(planes // group,), in_specs=[pl.Bloc...  5.76 us
    ppermute x1, starting transfers between devices, local(): rows = lax.ppermute(rotation, ('dom', 'st'), shift)  5.17 us
    pallas_call x1, Pallas kernels, rotate(): pl.pallas_call(rotate_kernel, grid=(points // tile,), in_specs=[pl.BlockS...  4.75 us
  transfers between devices with their start and end apart: 9, of which 6 were waited for; matrix products, arithmetic and copies ran while one was open for 1% of the time, Pallas kernels for 10%

profile of v1, /device:TPU:2, one launch (start us, length us, event | category | flops | bytes accessed | tf_op | source)
XLA Modules:
  0.0 102.3 jit_solution(342819683681589813)
XLA Ops:
  0.0 5.2 %collective-permute-start = (bf16[16,512]{1,0:T(8,128)(2,1)}, bf16[16,512]{1,0:T(8,128)(2,1)S(1)}, u32[]{:S(2)}, u32[]{:S(2)}) collective-permute-start(bf16[16,512]{1,0:T(8,128)(2,1)} %param.5), channel_id=1, source_target_pairs={{0,0},{1,1},{2,2},{3,3},{4,4},{5,5},{6,6},{7,7},{8,8},{9,9},{10,10... | collective-permute-start | bytes 49160 | tf_op jit(solution)/shard_map/ppermute | solution.py:382
  5.2 1.9 %edges.1 = (bf16[72,1024]{1,0:T(8,128)(2,1)}, bf16[72,1024]{1,0:T(8,128)(2,1)}) custom-call(bf16[16,64,1024]{2,1,0:T(8,128)(2,1)} %last_ref.1, bf16[16,64,1024]{2,1,0:T(8,128)(2,1)} %last_ref.1, bf16[64,1024]{1,0:T(8,128)(2,1)} %pot_last_ref.1, bf16[64,1024]{1,0:T(8,128)(2,1)} %pot_last_ref.1), custom_call_target="tpu_custom_call" | custom-call | tf_op jit(solution)/shard_map/edges/pallas_call | solution.py:68
  7.1 2.8 %collective-permute-start.1 = (bf16[72,1024]{1,0:T(8,128)(2,1)}, bf16[72,1024]{1,0:T(8,128)(2,1)S(1)}, u32[]{:S(2)}, u32[]{:S(2)}) collective-permute-start(bf16[72,1024]{1,0:T(8,128)(2,1)} %get-tuple-element.16), channel_id=1, source_target_pairs={{0,32},{32,64},{64,96},{96,128},{128,160},{160,192},{192,224},{1,3... | collective-permute-start | bytes 442376 | tf_op jit(solution)/shard_map/ppermute | solution.py:374
  9.9 2.7 %collective-permute-start.2 = (bf16[72,1024]{1,0:T(8,128)(2,1)}, bf16[72,1024]{1,0:T(8,128)(2,1)S(1)}, u32[]{:S(2)}, u32[]{:S(2)}) collective-permute-start(bf16[72,1024]{1,0:T(8,128)(2,1)} %get-tuple-element.17), channel_id=1, source_target_pairs={{32,0},{64,32},{96,64},{128,96},{160,128},{192,160},{224,192},{33,... | collective-permute-start | bytes 442376 | tf_op jit(solution)/shard_map/ppermute | solution.py:375
  12.7 5.8 %prepare.1 = (bf16[64,128,128]{2,1,0:T(8,128)(2,1)}, bf16[64,128,128]{2,1,0:T(8,128)(2,1)}) custom-call(bf16[16,64,1024]{2,1,0:T(8,128)(2,1)} %last_ref.1, bf16[64,1024]{1,0:T(8,128)(2,1)} %pot_last_ref.1), custom_call_target="tpu_custom_call" | custom-call | flops 2147483648 | bytes 8388608 | tf_op jit(solution)/shard_map/prepare/pallas_call | solution.py:108
  18.4 0.7 add_convert_fusion.edge_ref
  19.1 0.0 collective-permute-done.refs_0_
  19.1 0.0 collective-permute-done.1.low_ref
  19.1 0.0 copy-start.7
  19.1 0.0 collective-permute-done.2.high_ref
  19.1 0.6 copy-done.7
  19.8 0.1 copy-done.8
  19.8 16.1 %chebyshev.1 = bf16[32,16,2048]{2,1,0:T(8,128)(2,1)} custom-call(f32[2]{0:T(128)} %add_convert_fusion.edge_ref, bf16[64,128,128]{2,1,0:T(8,128)(2,1)} %get-tuple-element.14.field_hbm, bf16[64,128,128]{2,1,0:T(8,128)(2,1)} %get-tuple-element.15.pot_hbm, bf16[72,1024]{1,0:T(8,128)(2,1)} %copy-done.7, bf16[72,1024]{1,0:T(8,128)(2,1)} %copy-done.8), custom_call_target="tpu_custom_call" | custom-call | tf_op jit(solution)/shard_map/chebyshev/pallas_call | solution.py:291
  36.0 9.7 %all-to-all-start = ((bf16[32,16,2048]{2,1,0:T(8,128)(2,1)}), bf16[32,16,2048]{2,1,0:T(8,128)(2,1)S(1)}, u32[]{:S(2)}, u32[]{:S(2)}) async-start(bf16[32,16,2048]{2,1,0:T(8,128)(2,1)} %chebyshev.1), calls=%async_computation | async-start | bytes 4194304 | tf_op jit(solution)/shard_map/all_to_all | solution.py:388
  45.7 0.1 collective-permute-start.3
  45.8 1.1 %collective-permute-done.3.refs_1_ = bf16[16,512]{1,0:T(8,128)(2,1)S(1)} collective-permute-done((bf16[16,512]{1,0:T(8,128)(2,1)S(1)}, bf16[16,512]{1,0:T(8,128)(2,1)S(1)}, u32[]{:S(2)}, u32[]{:S(2)}) %collective-permute-start.3) | collective-permute-done | bytes 16416 | tf_op jit(solution)/shard_map/ppermute | solution.py:398
  46.9 1.9 %collective-permute-start.4 = (bf16[32,512]{1,0:T(8,128)(2,1)S(1)}, bf16[32,512]{1,0:T(8,128)(2,1)S(1)}, u32[]{:S(2)}, u32[]{:S(2)}) collective-permute-start(bf16[32,512]{1,0:T(8,128)(2,1)S(1)} %pad_maximum_fusion.2), channel_id=1, source_target_pairs={{0,64},{32,96},{64,128},{96,160},{128,192},{160,224},{192,0},{224,... | collective-permute-start | bytes 98312 | tf_op jit(solution)/shard_map/ppermute | solution.py:398
  48.9 2.0 %collective-permute-done.4.refs_2_ = bf16[32,512]{1,0:T(8,128)(2,1)S(1)} collective-permute-done((bf16[32,512]{1,0:T(8,128)(2,1)S(1)}, bf16[32,512]{1,0:T(8,128)(2,1)S(1)}, u32[]{:S(2)}, u32[]{:S(2)}) %collective-permute-start.4) | collective-permute-done | bytes 32800 | tf_op jit(solution)/shard_map/ppermute | solution.py:398
  50.9 1.5 %collective-permute-start.5 = (bf16[64,512]{1,0:T(8,128)(2,1)S(1)}, bf16[64,512]{1,0:T(8,128)(2,1)S(1)}, u32[]{:S(2)}, u32[]{:S(2)}) collective-permute-start(bf16[64,512]{1,0:T(8,128)(2,1)S(1)} %pad_maximum_fusion.1), channel_id=1, source_target_pairs={{0,128},{32,160},{64,192},{96,224},{128,0},{160,32},{192,64},{224,... | collective-permute-start | bytes 196616 | tf_op jit(solution)/shard_map/ppermute | solution.py:398
  52.3 4.4 %collective-permute-done.5.refs_3_ = bf16[64,512]{1,0:T(8,128)(2,1)S(1)} collective-permute-done((bf16[64,512]{1,0:T(8,128)(2,1)S(1)}, bf16[64,512]{1,0:T(8,128)(2,1)S(1)}, u32[]{:S(2)}, u32[]{:S(2)}) %collective-permute-start.5) | collective-permute-done | bytes 65568 | tf_op jit(solution)/shard_map/ppermute | solution.py:398
  56.7 1.9 %collective-permute-start.6 = (bf16[128,512]{1,0:T(8,128)(2,1)S(1)}, bf16[128,512]{1,0:T(8,128)(2,1)S(1)}, u32[]{:S(2)}, u32[]{:S(2)}) collective-permute-start(bf16[128,512]{1,0:T(8,128)(2,1)S(1)} %pad_maximum_fusion), channel_id=1, source_target_pairs={{0,8},{1,9},{2,10},{3,11},{4,12},{5,13},{6,14},{7,15},{8,16},{9,17... | collective-permute-start | bytes 393224 | tf_op jit(solution)/shard_map/ppermute | solution.py:398
  58.6 6.7 %collective-permute-done.6.refs_4_ = bf16[128,512]{1,0:T(8,128)(2,1)S(1)} collective-permute-done((bf16[128,512]{1,0:T(8,128)(2,1)S(1)}, bf16[128,512]{1,0:T(8,128)(2,1)S(1)}, u32[]{:S(2)}, u32[]{:S(2)}) %collective-permute-start.6) | collective-permute-done | bytes 131104 | tf_op jit(solution)/shard_map/ppermute | solution.py:398
  65.3 1.1 %collective-permute-start.7 = (bf16[256,512]{1,0:T(8,128)(2,1)S(1)}, bf16[256,512]{1,0:T(8,128)(2,1)S(1)}, u32[]{:S(2)}, u32[]{:S(2)}) collective-permute-start(bf16[256,512]{1,0:T(8,128)(2,1)S(1)} %constant_dynamic-update-slice_fusion), channel_id=1, source_target_pairs={{0,16},{1,17},{2,18},{3,19},{4,20},{5,21},{6,22},{7,23},{8,24},{9,... | collective-permute-start | bytes 786440 | tf_op jit(solution)/shard_map/ppermute | solution.py:398
  66.5 0.6 stack.24.place_ref
  67.0 12.7 %collective-permute-done.7.refs_5_ = bf16[256,512]{1,0:T(8,128)(2,1)S(1)} collective-permute-done((bf16[256,512]{1,0:T(8,128)(2,1)S(1)}, bf16[256,512]{1,0:T(8,128)(2,1)S(1)}, u32[]{:S(2)}, u32[]{:S(2)}) %collective-permute-start.7) | collective-permute-done | bytes 262176 | tf_op jit(solution)/shard_map/ppermute | solution.py:398
  79.8 0.0 copy-done.2
  79.8 0.0 copy-start.6
  79.8 0.7 copy-done.6
  80.5 2.3 %order.1.r_ref = bf16[512,512]{1,0:T(8,128)(2,1)} custom-call(s32[5]{0:T(128)} %stack.24.place_ref, bf16[16,512]{1,0:T(8,128)(2,1)} %copy-done.4, bf16[16,512]{1,0:T(8,128)(2,1)} %copy-done.5, bf16[32,512]{1,0:T(8,128)(2,1)} %copy-done.3, bf16[64,512]{1,0:T(8,128)(2,1)} %copy-done.1, bf16[128,512]{1,0:T(8,128)(2,1)} %copy-done.2, bf16[256,512]{1,0:T(8,128)(2,1)} %copy-done.6), custom_call_target="tpu_custom_call" | custom-call | tf_op jit(solution)/shard_map/order/pallas_call | solution.py:356
  82.8 13.4 %all-to-all-done = bf16[32,16,2048]{2,1,0:T(8,128)(2,1)S(1)} async-done(((bf16[32,16,2048]{2,1,0:T(8,128)(2,1)}), bf16[32,16,2048]{2,1,0:T(8,128)(2,1)S(1)}, u32[]{:S(2)}, u32[]{:S(2)}) %all-to-all-start) | async-done | bytes 2097184 | tf_op jit(solution)/shard_map/all_to_all | solution.py:388
  96.2 1.3 %copy-done = bf16[32,16,2048]{2,1,0:T(8,128)(2,1)} copy-done((bf16[32,16,2048]{2,1,0:T(8,128)(2,1)}, bf16[32,16,2048]{2,1,0:T(8,128)(2,1)S(1)}, u32[]{:S(2)}) %copy-start) | copy-done | bytes 2097176
  97.5 4.7 %rotate.1 = bf16[512,2048]{1,0:T(8,128)(2,1)} custom-call(bf16[512,512]{1,0:T(8,128)(2,1)} %order.1.r_ref, bf16[512,2048]{1,0:T(8,128)(2,1)} %bitcast.6), custom_call_target="tpu_custom_call" | custom-call | tf_op jit(solution)/shard_map/rotate/pallas_call | solution.py:318
  (19 shorter events, 0.1 us)
Async XLA Ops:
  0.0 19.1 %collective-permute-start = (bf16[16,512]{1,0:T(8,128)(2,1)}, bf16[16,512]{1,0:T(8,128)(2,1)S(1)}, u32[]{:S(2)}, u32[]{:S(2)}) collective-permute-start(bf16[16,512]{1,0:T(8,128)(2,1)} %param.5), channel_id=1, source_target_pairs={{0,0},{1,1},{2,2},{3,3},{4,4},{5,5},{6,6},{7,7},{8,8},{9,9},{10,10... | collective-permute-start | bytes 49160 | tf_op jit(solution)/shard_map/ppermute | solution.py:382
  7.1 12.0 %collective-permute-start.1 = (bf16[72,1024]{1,0:T(8,128)(2,1)}, bf16[72,1024]{1,0:T(8,128)(2,1)S(1)}, u32[]{:S(2)}, u32[]{:S(2)}) collective-permute-start(bf16[72,1024]{1,0:T(8,128)(2,1)} %get-tuple-element.16), channel_id=1, source_target_pairs={{0,32},{32,64},{64,96},{96,128},{128,160},{160,192},{192,224},{1,3... | collective-permute-start | bytes 442376 | tf_op jit(solution)/shard_map/ppermute | solution.py:374
  9.9 9.2 %collective-permute-start.2 = (bf16[72,1024]{1,0:T(8,128)(2,1)}, bf16[72,1024]{1,0:T(8,128)(2,1)S(1)}, u32[]{:S(2)}, u32[]{:S(2)}) collective-permute-start(bf16[72,1024]{1,0:T(8,128)(2,1)} %get-tuple-element.17), channel_id=1, source_target_pairs={{32,0},{64,32},{96,64},{128,96},{160,128},{192,160},{224,192},{33,... | collective-permute-start | bytes 442376 | tf_op jit(solution)/shard_map/ppermute | solution.py:375
  19.1 37.6 %copy-start.4 = (bf16[16,512]{1,0:T(8,128)(2,1)}, bf16[16,512]{1,0:T(8,128)(2,1)S(1)}, u32[]{:S(2)}) copy-start(bf16[16,512]{1,0:T(8,128)(2,1)S(1)} %collective-permute-done.refs_0_) | copy-start | bytes 49156
  19.1 0.7 copy-start.7
  19.1 0.7 copy-start.8
  36.0 60.2 %all-to-all-start = ((bf16[32,16,2048]{2,1,0:T(8,128)(2,1)}), bf16[32,16,2048]{2,1,0:T(8,128)(2,1)S(1)}, u32[]{:S(2)}, u32[]{:S(2)}) async-start(bf16[32,16,2048]{2,1,0:T(8,128)(2,1)} %chebyshev.1), calls=%async_computation | async-start | bytes 4194304 | tf_op jit(solution)/shard_map/all_to_all | solution.py:388
  45.7 1.3 %collective-permute-start.3 = (bf16[16,512]{1,0:T(8,128)(2,1)S(1)}, bf16[16,512]{1,0:T(8,128)(2,1)S(1)}, u32[]{:S(2)}, u32[]{:S(2)}) collective-permute-start(bf16[16,512]{1,0:T(8,128)(2,1)S(1)} %collective-permute-done.refs_0_), channel_id=1, source_target_pairs={{0,32},{32,0},{64,96},{96,64},{128,160},{160,128},{192,224},{224,1... | collective-permute-start | bytes 49160 | tf_op jit(solution)/shard_map/ppermute | solution.py:398
  46.9 32.8 %copy-start.5 = (bf16[16,512]{1,0:T(8,128)(2,1)}, bf16[16,512]{1,0:T(8,128)(2,1)S(1)}, u32[]{:S(2)}) copy-start(bf16[16,512]{1,0:T(8,128)(2,1)S(1)} %collective-permute-done.3.refs_1_) | copy-start | bytes 49156
  46.9 3.9 %collective-permute-start.4 = (bf16[32,512]{1,0:T(8,128)(2,1)S(1)}, bf16[32,512]{1,0:T(8,128)(2,1)S(1)}, u32[]{:S(2)}, u32[]{:S(2)}) collective-permute-start(bf16[32,512]{1,0:T(8,128)(2,1)S(1)} %pad_maximum_fusion.2), channel_id=1, source_target_pairs={{0,64},{32,96},{64,128},{96,160},{128,192},{160,224},{192,0},{224,... | collective-permute-start | bytes 98312 | tf_op jit(solution)/shard_map/ppermute | solution.py:398
  50.9 28.9 %copy-start.3 = (bf16[32,512]{1,0:T(8,128)(2,1)}, bf16[32,512]{1,0:T(8,128)(2,1)S(1)}, u32[]{:S(2)}) copy-start(bf16[32,512]{1,0:T(8,128)(2,1)S(1)} %collective-permute-done.4.refs_2_) | copy-start | bytes 98308
  50.9 5.9 %collective-permute-start.5 = (bf16[64,512]{1,0:T(8,128)(2,1)S(1)}, bf16[64,512]{1,0:T(8,128)(2,1)S(1)}, u32[]{:S(2)}, u32[]{:S(2)}) collective-permute-start(bf16[64,512]{1,0:T(8,128)(2,1)S(1)} %pad_maximum_fusion.1), channel_id=1, source_target_pairs={{0,128},{32,160},{64,192},{96,224},{128,0},{160,32},{192,64},{224,... | collective-permute-start | bytes 196616 | tf_op jit(solution)/shard_map/ppermute | solution.py:398
  56.7 23.0 %copy-start.1 = (bf16[64,512]{1,0:T(8,128)(2,1)}, bf16[64,512]{1,0:T(8,128)(2,1)S(1)}, u32[]{:S(2)}) copy-start(bf16[64,512]{1,0:T(8,128)(2,1)S(1)} %collective-permute-done.5.refs_3_) | copy-start | bytes 196612
  56.7 8.6 %collective-permute-start.6 = (bf16[128,512]{1,0:T(8,128)(2,1)S(1)}, bf16[128,512]{1,0:T(8,128)(2,1)S(1)}, u32[]{:S(2)}, u32[]{:S(2)}) collective-permute-start(bf16[128,512]{1,0:T(8,128)(2,1)S(1)} %pad_maximum_fusion), channel_id=1, source_target_pairs={{0,8},{1,9},{2,10},{3,11},{4,12},{5,13},{6,14},{7,15},{8,16},{9,17... | collective-permute-start | bytes 393224 | tf_op jit(solution)/shard_map/ppermute | solution.py:398
  65.3 14.5 %copy-start.2 = (bf16[128,512]{1,0:T(8,128)(2,1)}, bf16[128,512]{1,0:T(8,128)(2,1)S(1)}, u32[]{:S(2)}) copy-start(bf16[128,512]{1,0:T(8,128)(2,1)S(1)} %collective-permute-done.6.refs_4_) | copy-start | bytes 393220
  65.3 14.4 %collective-permute-start.7 = (bf16[256,512]{1,0:T(8,128)(2,1)S(1)}, bf16[256,512]{1,0:T(8,128)(2,1)S(1)}, u32[]{:S(2)}, u32[]{:S(2)}) collective-permute-start(bf16[256,512]{1,0:T(8,128)(2,1)S(1)} %constant_dynamic-update-slice_fusion), channel_id=1, source_target_pairs={{0,16},{1,17},{2,18},{3,19},{4,20},{5,21},{6,22},{7,23},{8,24},{9,... | collective-permute-start | bytes 786440 | tf_op jit(solution)/shard_map/ppermute | solution.py:398
  79.8 0.7 copy-start.6
  96.2 1.3 %copy-start = (bf16[32,16,2048]{2,1,0:T(8,128)(2,1)}, bf16[32,16,2048]{2,1,0:T(8,128)(2,1)S(1)}, u32[]{:S(2)}) copy-start(bf16[32,16,2048]{2,1,0:T(8,128)(2,1)S(1)} %all-to-all-done) | copy-start | bytes 6291460

commit v2 on v1

--- a/solution.py
+++ b/solution.py
@@ -76,6 +76,7 @@
         ],
         out_specs=[pl.BlockSpec(out.shape, lambda i: (0, 0))] * 2,
         out_shape=[out, out],
+        compiler_params=pltpu.CompilerParams(vmem_limit_bytes=8 << 20),
         name="edges",
     )(orbitals, orbitals, potential, potential)
 
@@ -117,13 +118,14 @@
         cost_estimate=pl.CostEstimate(
             flops=4 * 2 * states * planes * width * 256, transcendentals=0, bytes_accessed=8 << 20
         ),
+        compiler_params=pltpu.CompilerParams(vmem_limit_bytes=16 << 20),
         name="prepare",
     )(orbitals, potential)
 
 
 def filter_kernel(
-    edge_ref, field_hbm, pot_hbm, low_ref, high_ref, out_hbm,
-    even, odd, coef, field_ref, pot_ref, done_ref, out_ref, in_sems, out_sems,
+    field_ref, pot_ref, low_ref, high_ref, out_hbm,
+    even, odd, coef, done_ref, out_ref, out_sems,
 ):
     planes = field_ref.shape[0]
     owners, states, points = out_ref.shape
@@ -132,13 +134,8 @@
     b = 1.0 / cheb_scale
     runs = [(r, q) for r in range(INNER_Y) for q in range(NZ // 8)]
 
-    loads = [
-        pltpu.make_async_copy(field_hbm, field_ref, in_sems.at[0]),
-        pltpu.make_async_copy(pot_hbm, pot_ref, in_sems.at[1]),
-    ]
-    for load in loads:
-        load.start()
-
+    me, doms = lax.axis_index("dom"), lax.axis_size("dom")
+    flags = (jnp.where(me > 0, 1.0, 0.0), jnp.where(me < doms - 1, 1.0, 0.0))
     def scaled(p):
         return (p - (cheb_shift - 3.0)) * 2.0
 
@@ -172,9 +169,6 @@
             both = scaled(turned(stacked(pot, states, at + p, 2)))
             coef[base + p] = both[:, :LANES]
             coef[base + p + 1] = both[:, LANES:]
-
-    for load in loads:
-        load.wait()
 
     def fill(i, carry):
         for r in range(2):
@@ -224,15 +218,16 @@
         for r, q in runs:
             dst[pl.ds(base + (r * RUN + 8 + q * 8), 8), :] = results[r, q]
 
-    unroll = 4
+    unroll = 8
     for k in range(1, DEGREE):
-        def outer(side, plane, carry, k=k):
-            flag = edge_ref[side]
-            store(k, plane, {rq: v * flag for rq, v in step(k, plane).items()})
+        def outer(i, carry, k=k):
+            both = (k + i, halo + planes + i)
+            results = [step(k, plane) for plane in both]
+            for plane, flag, res in zip(both, flags, results):
+                store(k, plane, {rq: v * flag for rq, v in res.items()})
             return carry
 
-        lax.fori_loop(k, halo, functools.partial(outer, 0), 0)
-        lax.fori_loop(halo + planes, 2 * halo + planes - k, functools.partial(outer, 1), 0)
+        lax.fori_loop(0, halo - k, outer, 0)
 
         def body(i, carry, k=k):
             results = [step(k, halo + unroll * i + r) for r in range(unroll)]
@@ -282,50 +277,67 @@
         send(i).wait()
 
 
-def chebyshev(field, pot, low, high, edge, owners, states):
+def chebyshev(field, pot, low, high, owners, states):
     planes = field.shape[0]
     points = planes * LANES * LANES // states // owners
     total = planes + 2 * DEGREE
-    vmem = pl.BlockSpec(memory_space=pltpu.VMEM)
     anywhere = pl.BlockSpec(memory_space=pl.ANY)
     return pl.pallas_call(
         filter_kernel,
-        in_specs=[pl.BlockSpec(memory_space=pltpu.SMEM), anywhere, anywhere, vmem, vmem],
+        in_specs=[pl.BlockSpec(memory_space=pltpu.VMEM)] * 4,
         out_specs=anywhere,
         out_shape=jax.ShapeDtypeStruct((owners, states, points), BF16),
         scratch_shapes=[
             pltpu.VMEM((total * PLANE + 8, LANES), F32),
             pltpu.VMEM((total * PLANE + 8, LANES), F32),
             pltpu.VMEM((total, LANES, LANES), F32),
-            pltpu.VMEM(field.shape, BF16),
-            pltpu.VMEM(pot.shape, BF16),
             pltpu.VMEM((planes * LANES, LANES), BF16),
             pltpu.VMEM((owners, states, points), BF16),
-            pltpu.SemaphoreType.DMA((2,)),
-            pltpu.SemaphoreType.DMA((planes // 4,)),
+            pltpu.SemaphoreType.DMA((planes // 8,)),
         ],
+        compiler_params=pltpu.CompilerParams(vmem_limit_bytes=32 << 20),
         name="chebyshev",
-    )(edge, field, pot, low, high)
-
-
-def rotate_kernel(r_ref, f_ref, out_ref):
-    out_ref[...] = jnp.dot(r_ref[...], f_ref[...], preferred_element_type=F32).astype(BF16)
+    )(*in_vmem(field, pot, low, high))
+
+
+def rotate_kernel(r_ref, f_ref, out_hbm, out_ref, out_sems):
+    tiles = out_ref.shape[0]
+    tile = out_ref.shape[2]
+
+    def give(i):
+        return pltpu.make_async_copy(
+            out_ref.at[i], out_hbm.at[:, pl.ds(i * tile, tile)], out_sems.at[i]
+        )
+
+    for i in range(tiles):
+        part = f_ref[:, i * tile : (i + 1) * tile]
+        out_ref[i] = jnp.dot(r_ref[...], part, preferred_element_type=F32).astype(BF16)
+        give(i).start()
+    for i in range(tiles):
+        give(i).wait()
+
+
+def in_vmem(*arrays):
+    return [pltpu.with_memory_space_constraint(a, pltpu.VMEM) for a in arrays]
 
 
 def rotate(rotation, filtered):
     total, points = filtered.shape
-    tile = 512
+    tile = 256
+    tiles = points // tile
+    vmem = pl.BlockSpec(memory_space=pltpu.VMEM)
     return pl.pallas_call(
         rotate_kernel,
-        grid=(points // tile,),
-        in_specs=[
-            pl.BlockSpec(rotation.shape, lambda i: (0, 0)),
-            pl.BlockSpec((total, tile), lambda i: (0, i)),
+        in_specs=[vmem, vmem],
+        out_specs=pl.BlockSpec(memory_space=pl.ANY),
+        out_shape=jax.ShapeDtypeStruct((rotation.shape[0], points), BF16),
+        scratch_shapes=[
+            pltpu.VMEM((tiles, rotation.shape[0], tile), BF16),
+            pltpu.SemaphoreType.DMA((tiles,)),
         ],
-        out_specs=pl.BlockSpec((rotation.shape[0], tile), lambda i: (0, i)),
-        out_shape=jax.ShapeDtypeStruct((rotation.shape[0], points), BF16),
+        compiler_params=pltpu.CompilerParams(vmem_limit_bytes=12 << 20),
         name="rotate",
-    )(rotation, filtered)
+    )(*in_vmem(rotation, filtered))
 
 
 def order_kernel(place_ref, *refs):
@@ -358,6 +370,7 @@
         in_specs=[pl.BlockSpec(memory_space=pltpu.SMEM)] + [vmem] * len(parts),
         out_specs=vmem,
         out_shape=jax.ShapeDtypeStruct((total, cols), BF16),
+        compiler_params=pltpu.CompilerParams(vmem_limit_bytes=8 << 20),
         name="order",
     )(place, *parts)
 
@@ -370,6 +383,8 @@
     me, spot = lax.axis_index("dom"), lax.axis_index("st")
     up = [(i, i + 1) for i in range(doms - 1)]
     down = [(i + 1, i) for i in range(doms - 1)]
+    orbitals = pltpu.with_memory_space_constraint(orbitals, pltpu.HBM)
+    potential = pltpu.with_memory_space_constraint(potential, pltpu.HBM)
     low_send, high_send = edges(orbitals, potential)
     low = lax.ppermute(high_send, "dom", up)
     high = lax.ppermute(low_send, "dom", down)
@@ -379,11 +394,11 @@
         for y in range(ys)
         for z in range(zs)
     ]
+    rotation, low_send = lax.optimization_barrier((rotation, low_send))
     rows = lax.ppermute(rotation, ("dom", "st"), shift)
     field, pot = prepare(orbitals, potential)
     rows, field = lax.optimization_barrier((rows, field))
-    edge = jnp.stack([me > 0, me < doms - 1]).astype(F32)
-    filtered = chebyshev(field, pot, low, high, edge, owners, states)
+    filtered = chebyshev(field, pot, low, high, owners, states)
     rows, _ = lax.optimization_barrier((rows, filtered))
     regrouped = lax.all_to_all(filtered, "st", split_axis=0, concat_axis=0, tiled=True)
     parts = [rows]

time: 103 us -> 92.2 us (0.90)
  Pallas kernels: 30.9 us -> 21.3 us
  waiting for transfers between devices: 40.3 us -> 45.9 us
  starting transfers between devices: 27 us -> 23.6 us
  local copies, waits for them, and re-layouts: 3.35 us -> 0.11 us
    pallas_call x2, Pallas kernels: 20.9 us -> 14.5 us  [the longest x1 12.4 us: chebyshev(): pl.pallas_call(filter_kernel, in_specs=[pl.BlockSpec(memory_space=pltpu.V...]
    ppermute x5, waiting for transfers between devices: 26.9 us -> 31 us  [local(): lax.ppermute(parts[0] if len(parts) == 1 else jnp.concatenate(parts), axi...]
    unnamed x22 -> x6, local copies, waits for them, and re-layouts: 2.77 us -> 0.02 us
    ppermute x5, starting transfers between devices: 6.56 us -> 4.18 us  [local(): lax.ppermute(parts[0] if len(parts) == 1 else jnp.concatenate(parts), axi...]
    all_to_all x1, waiting for transfers between devices: 13.4 us -> 14.9 us  [local(): lax.all_to_all(filtered, 'st', split_axis=0, concat_axis=0, tiled=True)]
    pallas_call x1, Pallas kernels: 2.35 us -> 0.97 us  [ordered(): pl.pallas_call(order_kernel, in_specs=[pl.BlockSpec(memory_space=pltpu.SM...]
    pallas_call x1, Pallas kernels: 5.76 us -> 4.56 us  [prepare(): pl.pallas_call(prepare_kernel, grid=(planes // group,), in_specs=[pl.Bloc...]
  transfers between devices with their start and end apart: 9 -> 9, of which waited for: 6 -> 6; matrix products, arithmetic and copies ran while one was open for 1% -> 0% of each run, Pallas kernels for 10% -> 6%
where the time goes in v2:
time: 92.2 us; the launch traced here: 91 us
  waiting for transfers between devices  45.9 us (50%)
  starting transfers between devices  23.6 us (26%)
  Pallas kernels  21.3 us (23%)
    ppermute x5, waiting for transfers between devices, local(): lax.ppermute(parts[0] if len(parts) == 1 else jnp.concatenate(parts), axi...  31 us
    all_to_all x1, waiting for transfers between devices, local(): lax.all_to_all(filtered, 'st', split_axis=0, concat_axis=0, tiled=True)  14.9 us
    pallas_call x1, Pallas kernels, chebyshev(): pl.pallas_call(filter_kernel, in_specs=[pl.BlockSpec(memory_space=pltpu.V...  12.4 us
    all_to_all x1, starting transfers between devices, local(): lax.all_to_all(filtered, 'st', split_axis=0, concat_axis=0, tiled=True)  8.8 us
    ppermute x1, starting transfers between devices, local(): rows = lax.ppermute(rotation, ('dom', 'st'), shift)  5.18 us
    pallas_call x1, Pallas kernels, prepare(): pl.pallas_call(prepare_kernel, grid=(planes // group,), in_specs=[pl.Bloc...  4.56 us
    ppermute x5, starting transfers between devices, local(): lax.ppermute(parts[0] if len(parts) == 1 else jnp.concatenate(parts), axi...  4.18 us
    ppermute x1, starting transfers between devices, local(): low = lax.ppermute(high_send, 'dom', up)  3.48 us
  transfers between devices with their start and end apart: 9, of which 6 were waited for; matrix products, arithmetic and copies ran while one was open for 0% of the time, Pallas kernels for 6%

profile of v2, /device:TPU:2, one launch (start us, length us, event | category | flops | bytes accessed | tf_op | source)
XLA Modules:
  0.0 91.0 jit_solution(6357719159488050807)
XLA Ops:
  0.0 0.0 copy-start
  0.0 1.3 %edges.1 = (bf16[72,1024]{1,0:T(8,128)(2,1)S(1)}, bf16[72,1024]{1,0:T(8,128)(2,1)S(1)}) custom-call(bf16[16,64,1024]{2,1,0:T(8,128)(2,1)} %x_ref.1, bf16[16,64,1024]{2,1,0:T(8,128)(2,1)} %x_ref.1, bf16[64,1024]{1,0:T(8,128)(2,1)} %pot_ref.1, bf16[64,1024]{1,0:T(8,128)(2,1)} %pot_ref.1), custom_call_target="tpu_custom_call" | custom-call | tf_op jit(solution)/shard_map/edges/pallas_call | solution.py:68
  1.3 1.9 %collective-permute-start.2 = (bf16[72,1024]{1,0:T(8,128)(2,1)S(1)}, bf16[72,1024]{1,0:T(8,128)(2,1)S(1)}, u32[]{:S(2)}, u32[]{:S(2)}) collective-permute-start(bf16[72,1024]{1,0:T(8,128)(2,1)S(1)} %get-tuple-element.13), channel_id=1, source_target_pairs={{32,0},{64,32},{96,64},{128,96},{160,128},{192,160},{224,192},{33,... | collective-permute-start | bytes 442376 | tf_op jit(solution)/shard_map/ppermute | solution.py:390
  3.2 0.0 copy-done
  3.2 5.2 %collective-permute-start = (bf16[16,512]{1,0:T(8,128)(2,1)S(1)}, bf16[16,512]{1,0:T(8,128)(2,1)S(1)}, u32[]{:S(2)}, u32[]{:S(2)}) collective-permute-start(bf16[16,512]{1,0:T(8,128)(2,1)S(1)} %copy-done), channel_id=1, source_target_pairs={{0,0},{1,1},{2,2},{3,3},{4,4},{5,5},{6,6},{7,7},{8,8},{9,9},{10,10... | collective-permute-start | bytes 49160 | tf_op jit(solution)/shard_map/ppermute | solution.py:398
  8.4 3.5 %collective-permute-start.1 = (bf16[72,1024]{1,0:T(8,128)(2,1)S(1)}, bf16[72,1024]{1,0:T(8,128)(2,1)S(1)}, u32[]{:S(2)}, u32[]{:S(2)}) collective-permute-start(bf16[72,1024]{1,0:T(8,128)(2,1)S(1)} %get-tuple-element.19), channel_id=1, source_target_pairs={{0,32},{32,64},{64,96},{96,128},{128,160},{160,192},{192,224},{1,3... | collective-permute-start | bytes 442376 | tf_op jit(solution)/shard_map/ppermute | solution.py:389
  11.9 4.6 %prepare.1 = (bf16[64,128,128]{2,1,0:T(8,128)(2,1)S(1)}, bf16[64,128,128]{2,1,0:T(8,128)(2,1)S(1)}) custom-call(bf16[16,64,1024]{2,1,0:T(8,128)(2,1)} %x_ref.1, bf16[64,1024]{1,0:T(8,128)(2,1)} %pot_ref.1), custom_call_target="tpu_custom_call" | custom-call | flops 2147483648 | bytes 8388608 | tf_op jit(solution)/shard_map/prepare/pallas_call | solution.py:109
  16.5 0.0 collective-permute-done.refs_0_
  16.5 0.0 collective-permute-done.2.high_ref
  16.5 0.0 collective-permute-done.1.low_ref
  16.5 12.4 %chebyshev.1 = bf16[32,16,2048]{2,1,0:T(8,128)(2,1)} custom-call(bf16[64,128,128]{2,1,0:T(8,128)(2,1)S(1)} %get-tuple-element.17.field_ref, bf16[64,128,128]{2,1,0:T(8,128)(2,1)S(1)} %get-tuple-element.18.pot_ref, bf16[72,1024]{1,0:T(8,128)(2,1)S(1)} %collective-permute-done.1.low_ref, bf16[72,1024]{1,0:T(8,128)(2,1)S(1)} %collective-permute-done.2.high_ref), custom_call_target="tpu_custom_call" | custom-call | tf_op jit(solution)/shard_map/chebyshev/pallas_call | solution.py:285
  28.9 8.8 %all-to-all-start = ((bf16[32,16,2048]{2,1,0:T(8,128)(2,1)}), bf16[32,16,2048]{2,1,0:T(8,128)(2,1)S(1)}, u32[]{:S(2)}, u32[]{:S(2)}) async-start(bf16[32,16,2048]{2,1,0:T(8,128)(2,1)} %chebyshev.1), calls=%async_computation | async-start | bytes 4194304 | tf_op jit(solution)/shard_map/all_to_all | solution.py:403
  37.7 1.2 %collective-permute-start.3 = (bf16[16,512]{1,0:T(8,128)(2,1)S(1)}, bf16[16,512]{1,0:T(8,128)(2,1)S(1)}, u32[]{:S(2)}, u32[]{:S(2)}) collective-permute-start(bf16[16,512]{1,0:T(8,128)(2,1)S(1)} %collective-permute-done.refs_0_), channel_id=1, source_target_pairs={{0,32},{32,0},{64,96},{96,64},{128,160},{160,128},{192,224},{224,1... | collective-permute-start | bytes 49160 | tf_op jit(solution)/shard_map/ppermute | solution.py:413
  38.8 0.8 collective-permute-done.3.refs_1_
  39.7 0.5 collective-permute-start.4
  40.2 3.4 %collective-permute-done.4.refs_2_ = bf16[32,512]{1,0:T(8,128)(2,1)S(1)} collective-permute-done((bf16[32,512]{1,0:T(8,128)(2,1)S(1)}, bf16[32,512]{1,0:T(8,128)(2,1)S(1)}, u32[]{:S(2)}, u32[]{:S(2)}) %collective-permute-start.4) | collective-permute-done | bytes 32800 | tf_op jit(solution)/shard_map/ppermute | solution.py:413
  43.6 0.0 collective-permute-start.5
  43.7 5.7 %collective-permute-done.5.refs_3_ = bf16[64,512]{1,0:T(8,128)(2,1)S(1)} collective-permute-done((bf16[64,512]{1,0:T(8,128)(2,1)S(1)}, bf16[64,512]{1,0:T(8,128)(2,1)S(1)}, u32[]{:S(2)}, u32[]{:S(2)}) %collective-permute-start.5) | collective-permute-done | bytes 65568 | tf_op jit(solution)/shard_map/ppermute | solution.py:413
  49.4 1.6 %collective-permute-start.6 = (bf16[128,512]{1,0:T(8,128)(2,1)S(1)}, bf16[128,512]{1,0:T(8,128)(2,1)S(1)}, u32[]{:S(2)}, u32[]{:S(2)}) collective-permute-start(bf16[128,512]{1,0:T(8,128)(2,1)S(1)} %pad_maximum_fusion), channel_id=1, source_target_pairs={{0,8},{1,9},{2,10},{3,11},{4,12},{5,13},{6,14},{7,15},{8,16},{9,17... | collective-permute-start | bytes 393224 | tf_op jit(solution)/shard_map/ppermute | solution.py:413
  51.0 6.6 %collective-permute-done.6.refs_4_ = bf16[128,512]{1,0:T(8,128)(2,1)S(1)} collective-permute-done((bf16[128,512]{1,0:T(8,128)(2,1)S(1)}, bf16[128,512]{1,0:T(8,128)(2,1)S(1)}, u32[]{:S(2)}, u32[]{:S(2)}) %collective-permute-start.6) | collective-permute-done | bytes 131104 | tf_op jit(solution)/shard_map/ppermute | solution.py:413
  57.6 0.8 collective-permute-start.7
  58.4 0.1 stack.15.place_ref
  58.5 14.5 %collective-permute-done.7.refs_5_ = bf16[256,512]{1,0:T(8,128)(2,1)S(1)} collective-permute-done((bf16[256,512]{1,0:T(8,128)(2,1)S(1)}, bf16[256,512]{1,0:T(8,128)(2,1)S(1)}, u32[]{:S(2)}, u32[]{:S(2)}) %collective-permute-start.7) | collective-permute-done | bytes 262176 | tf_op jit(solution)/shard_map/ppermute | solution.py:413
  73.0 1.0 %order.1.r_ref = bf16[512,512]{1,0:T(8,128)(2,1)S(1)} custom-call(s32[5]{0:T(128)S(1)} %stack.15.place_ref, bf16[16,512]{1,0:T(8,128)(2,1)S(1)} %collective-permute-done.refs_0_, bf16[16,512]{1,0:T(8,128)(2,1)S(1)} %collective-permute-done.3.refs_1_, bf16[32,512]{1,0:T(8,128)(2,1)S(1)} %collective-permute-done.4.refs_2_, ...), custom_call_target="tpu_custom_call" | custom-call | tf_op jit(solution)/shard_map/order/pallas_call | solution.py:368
  74.0 14.9 %all-to-all-done = bf16[32,16,2048]{2,1,0:T(8,128)(2,1)S(1)} async-done(((bf16[32,16,2048]{2,1,0:T(8,128)(2,1)}), bf16[32,16,2048]{2,1,0:T(8,128)(2,1)S(1)}, u32[]{:S(2)}, u32[]{:S(2)}) %all-to-all-start) | async-done | bytes 2097184 | tf_op jit(solution)/shard_map/all_to_all | solution.py:403
  88.8 2.2 %rotate.1 = bf16[512,2048]{1,0:T(8,128)(2,1)} custom-call(bf16[512,512]{1,0:T(8,128)(2,1)S(1)} %order.1.r_ref, bf16[512,2048]{1,0:T(8,128)(2,1)S(1)} %bitcast.4), custom_call_target="tpu_custom_call" | custom-call | tf_op jit(solution)/shard_map/rotate/pallas_call | solution.py:329
  (8 shorter events, 0.0 us)
Async XLA Ops:
  0.0 3.2 %copy-start = (bf16[16,512]{1,0:T(8,128)(2,1)S(1)}, bf16[16,512]{1,0:T(8,128)(2,1)}, u32[]{:S(2)}) copy-start(bf16[16,512]{1,0:T(8,128)(2,1)} %param.5) | copy-start | bytes 49156
  1.3 15.2 %collective-permute-start.2 = (bf16[72,1024]{1,0:T(8,128)(2,1)S(1)}, bf16[72,1024]{1,0:T(8,128)(2,1)S(1)}, u32[]{:S(2)}, u32[]{:S(2)}) collective-permute-start(bf16[72,1024]{1,0:T(8,128)(2,1)S(1)} %get-tuple-element.13), channel_id=1, source_target_pairs={{32,0},{64,32},{96,64},{128,96},{160,128},{192,160},{224,192},{33,... | collective-permute-start | bytes 442376 | tf_op jit(solution)/shard_map/ppermute | solution.py:390
  3.2 13.2 %collective-permute-start = (bf16[16,512]{1,0:T(8,128)(2,1)S(1)}, bf16[16,512]{1,0:T(8,128)(2,1)S(1)}, u32[]{:S(2)}, u32[]{:S(2)}) collective-permute-start(bf16[16,512]{1,0:T(8,128)(2,1)S(1)} %copy-done), channel_id=1, source_target_pairs={{0,0},{1,1},{2,2},{3,3},{4,4},{5,5},{6,6},{7,7},{8,8},{9,9},{10,10... | collective-permute-start | bytes 49160 | tf_op jit(solution)/shard_map/ppermute | solution.py:398
  8.4 8.1 %collective-permute-start.1 = (bf16[72,1024]{1,0:T(8,128)(2,1)S(1)}, bf16[72,1024]{1,0:T(8,128)(2,1)S(1)}, u32[]{:S(2)}, u32[]{:S(2)}) collective-permute-start(bf16[72,1024]{1,0:T(8,128)(2,1)S(1)} %get-tuple-element.19), channel_id=1, source_target_pairs={{0,32},{32,64},{64,96},{96,128},{128,160},{160,192},{192,224},{1,3... | collective-permute-start | bytes 442376 | tf_op jit(solution)/shard_map/ppermute | solution.py:389
  28.9 60.0 %all-to-all-start = ((bf16[32,16,2048]{2,1,0:T(8,128)(2,1)}), bf16[32,16,2048]{2,1,0:T(8,128)(2,1)S(1)}, u32[]{:S(2)}, u32[]{:S(2)}) async-start(bf16[32,16,2048]{2,1,0:T(8,128)(2,1)} %chebyshev.1), calls=%async_computation | async-start | bytes 4194304 | tf_op jit(solution)/shard_map/all_to_all | solution.py:403
  37.7 2.0 %collective-permute-start.3 = (bf16[16,512]{1,0:T(8,128)(2,1)S(1)}, bf16[16,512]{1,0:T(8,128)(2,1)S(1)}, u32[]{:S(2)}, u32[]{:S(2)}) collective-permute-start(bf16[16,512]{1,0:T(8,128)(2,1)S(1)} %collective-permute-done.refs_0_), channel_id=1, source_target_pairs={{0,32},{32,0},{64,96},{96,64},{128,160},{160,128},{192,224},{224,1... | collective-permute-start | bytes 49160 | tf_op jit(solution)/shard_map/ppermute | solution.py:413
  39.7 3.9 %collective-permute-start.4 = (bf16[32,512]{1,0:T(8,128)(2,1)S(1)}, bf16[32,512]{1,0:T(8,128)(2,1)S(1)}, u32[]{:S(2)}, u32[]{:S(2)}) collective-permute-start(bf16[32,512]{1,0:T(8,128)(2,1)S(1)} %pad_maximum_fusion.2), channel_id=1, source_target_pairs={{0,64},{32,96},{64,128},{96,160},{128,192},{160,224},{192,0},{224,... | collective-permute-start | bytes 98312 | tf_op jit(solution)/shard_map/ppermute | solution.py:413
  43.6 5.8 %collective-permute-start.5 = (bf16[64,512]{1,0:T(8,128)(2,1)S(1)}, bf16[64,512]{1,0:T(8,128)(2,1)S(1)}, u32[]{:S(2)}, u32[]{:S(2)}) collective-permute-start(bf16[64,512]{1,0:T(8,128)(2,1)S(1)} %pad_maximum_fusion.1), channel_id=1, source_target_pairs={{0,128},{32,160},{64,192},{96,224},{128,0},{160,32},{192,64},{224,... | collective-permute-start | bytes 196616 | tf_op jit(solution)/shard_map/ppermute | solution.py:413
  49.4 8.2 %collective-permute-start.6 = (bf16[128,512]{1,0:T(8,128)(2,1)S(1)}, bf16[128,512]{1,0:T(8,128)(2,1)S(1)}, u32[]{:S(2)}, u32[]{:S(2)}) collective-permute-start(bf16[128,512]{1,0:T(8,128)(2,1)S(1)} %pad_maximum_fusion), channel_id=1, source_target_pairs={{0,8},{1,9},{2,10},{3,11},{4,12},{5,13},{6,14},{7,15},{8,16},{9,17... | collective-permute-start | bytes 393224 | tf_op jit(solution)/shard_map/ppermute | solution.py:413
  57.6 15.4 %collective-permute-start.7 = (bf16[256,512]{1,0:T(8,128)(2,1)S(1)}, bf16[256,512]{1,0:T(8,128)(2,1)S(1)}, u32[]{:S(2)}, u32[]{:S(2)}) collective-permute-start(bf16[256,512]{1,0:T(8,128)(2,1)S(1)} %constant_dynamic-update-slice_fusion), channel_id=1, source_target_pairs={{0,16},{1,17},{2,18},{3,19},{4,20},{5,21},{6,22},{7,23},{8,24},{9,... | collective-permute-start | bytes 786440 | tf_op jit(solution)/shard_map/ppermute | solution.py:413

commit v3 on v2

--- a/solution.py
+++ b/solution.py
@@ -87,19 +87,33 @@
     return jnp.dot(repeat, pot_rows, preferred_element_type=F32).astype(BF16)
 
 
-def prepare_kernel(x_ref, pot_ref, field_ref, pot_out_ref):
+def prepare_kernel(x_ref, pot_ref, field_ref, pot_out_ref, select):
     states, group, width = x_ref.shape
+    tiles = width // LANES
+
+    @pl.when(pl.program_id(0) == 0)
+    def _():
+        r = lax.broadcasted_iota(jnp.int32, select.shape, 0)
+        col = lax.broadcasted_iota(jnp.int32, select.shape, 1)
+        want = (col % LANES) // states * group + col // LANES
+        select[...] = jnp.where(r == want, 1.0, 0.0).astype(BF16)
+
     pick = one_hot(
         states * group, states * group, lambda r: (r % states) * group + r // states
     )
     rows = x_ref[...].reshape(states * group, width)
+    pot = jnp.concatenate(
+        [pot_ref[:, j * LANES : (j + 1) * LANES] for j in range(tiles)], axis=0
+    )
+    pot = turned(pot).astype(BF16)
     rows = jnp.dot(pick, rows, preferred_element_type=F32).astype(BF16)
-    pot = spread(pot_ref[...], states)
     for p in range(0, group, 2):
-        for source, target in ((rows, field_ref), (pot, pot_out_ref)):
-            both = turned(stacked(source, states, p, 2)).astype(BF16)
-            target[p] = both[:, :LANES]
-            target[p + 1] = both[:, LANES:]
+        at = slice(p * LANES, (p + 2) * LANES)
+        spreads = jnp.dot(pot, select[:, at], preferred_element_type=F32).astype(BF16)
+        both = turned(stacked(rows, states, p, 2)).astype(BF16)
+        for source, target in ((both, field_ref), (spreads, pot_out_ref)):
+            target[p] = source[:, :LANES]
+            target[p + 1] = source[:, LANES:]
 
 
 def prepare(orbitals, potential):
@@ -115,6 +129,7 @@
         ],
         out_specs=[pl.BlockSpec((group, LANES, LANES), lambda i: (i, 0, 0))] * 2,
         out_shape=[out, out],
+        scratch_shapes=[pltpu.VMEM((group * width // LANES, group * LANES), BF16)],
         cost_estimate=pl.CostEstimate(
             flops=4 * 2 * states * planes * width * 256, transcendentals=0, bytes_accessed=8 << 20
         ),
@@ -170,14 +185,9 @@
             coef[base + p] = both[:, :LANES]
             coef[base + p + 1] = both[:, LANES:]
 
-    def fill(i, carry):
-        for r in range(2):
-            p = i * 2 + r
-            put(even, halo + p, field_ref[p].astype(F32))
-            coef[halo + p] = scaled(pot_ref[p].astype(F32))
-        return carry
-
-    lax.fori_loop(0, planes // 2, fill, 0)
+    for p in range(planes):
+        put(even, halo + p, field_ref[p].astype(F32))
+        coef[halo + p] = scaled(pot_ref[p].astype(F32))
 
     lane = lax.broadcasted_iota(jnp.int32, (8, LANES), 1)
     first_y = lane < states
@@ -383,9 +393,10 @@
     me, spot = lax.axis_index("dom"), lax.axis_index("st")
     up = [(i, i + 1) for i in range(doms - 1)]
     down = [(i + 1, i) for i in range(doms - 1)]
-    orbitals = pltpu.with_memory_space_constraint(orbitals, pltpu.HBM)
-    potential = pltpu.with_memory_space_constraint(potential, pltpu.HBM)
-    low_send, high_send = edges(orbitals, potential)
+    low_send, high_send = edges(
+        pltpu.with_memory_space_constraint(orbitals, pltpu.HBM),
+        pltpu.with_memory_space_constraint(potential, pltpu.HBM),
+    )
     low = lax.ppermute(high_send, "dom", up)
     high = lax.ppermute(low_send, "dom", down)
     shift = [

time: 92.2 us -> 89.9 us (0.975); the launches traced: 91 us -> 89.7 us
  starting transfers between devices: 23.6 us -> 26.8 us
  waiting for transfers between devices: 45.9 us -> 42.9 us
  Pallas kernels: 21.3 us -> 19.7 us
    ppermute x5, starting transfers between devices: 4.18 us -> 6.68 us  [local(): lax.ppermute(parts[0] if len(parts) == 1 else jnp.concatenate(parts), axi...]
    ppermute x5, waiting for transfers between devices: 31 us -> 28.6 us  [local(): lax.ppermute(parts[0] if len(parts) == 1 else jnp.concatenate(parts), axi...]
    pallas_call x1, Pallas kernels: 4.56 us -> 3.02 us  [prepare(): pl.pallas_call(prepare_kernel, grid=(planes // group,), in_specs=[pl.Bloc...]
  transfers between devices with their start and end apart: 9 -> 9, of which waited for: 6 -> 6; matrix products, arithmetic and copies ran while one was open for 0% -> 0% of each run, Pallas kernels for 6% -> 4%
where the time goes in v3:
time: 89.9 us; the launch traced here: 89.7 us
  waiting for transfers between devices  42.9 us (48%)
  starting transfers between devices  26.8 us (30%)
  Pallas kernels  19.7 us (22%)
    ppermute x5, waiting for transfers between devices, local(): lax.ppermute(parts[0] if len(parts) == 1 else jnp.concatenate(parts), axi...  28.6 us
    all_to_all x1, waiting for transfers between devices, local(): lax.all_to_all(filtered, 'st', split_axis=0, concat_axis=0, tiled=True)  14.2 us
    pallas_call x1, Pallas kernels, chebyshev(): pl.pallas_call(filter_kernel, in_specs=[pl.BlockSpec(memory_space=pltpu.V...  12.1 us
    all_to_all x1, starting transfers between devices, local(): lax.all_to_all(filtered, 'st', split_axis=0, concat_axis=0, tiled=True)  9.57 us
    ppermute x5, starting transfers between devices, local(): lax.ppermute(parts[0] if len(parts) == 1 else jnp.concatenate(parts), axi...  6.68 us
    ppermute x1, starting transfers between devices, local(): rows = lax.ppermute(rotation, ('dom', 'st'), shift)  5.18 us
    ppermute x1, starting transfers between devices, local(): low = lax.ppermute(high_send, 'dom', up)  3.48 us
    pallas_call x1, Pallas kernels, prepare(): pl.pallas_call(prepare_kernel, grid=(planes // group,), in_specs=[pl.Bloc...  3.02 us
  transfers between devices with their start and end apart: 9, of which 6 were waited for; matrix products, arithmetic and copies ran while one was open for 0% of the time, Pallas kernels for 4%

profile of v3, /device:TPU:2, one launch (start us, length us, event | category | flops | bytes accessed | tf_op | source)
XLA Modules:
  0.0 89.7 jit_solution(15374069415259875584)
XLA Ops:
  0.0 0.0 copy-start
  0.0 0.0 copy-start.1
  0.0 0.0 copy-start.2
  0.0 1.4 %edges.1 = (bf16[72,1024]{1,0:T(8,128)(2,1)S(1)}, bf16[72,1024]{1,0:T(8,128)(2,1)S(1)}) custom-call(bf16[16,64,1024]{2,1,0:T(8,128)(2,1)} %x_ref.1, bf16[16,64,1024]{2,1,0:T(8,128)(2,1)} %x_ref.1, bf16[64,1024]{1,0:T(8,128)(2,1)} %pot_ref.1, bf16[64,1024]{1,0:T(8,128)(2,1)} %pot_ref.1), custom_call_target="tpu_custom_call" | custom-call | tf_op jit(solution)/shard_map/edges/pallas_call | solution.py:68
  1.4 1.9 %collective-permute-start.2 = (bf16[72,1024]{1,0:T(8,128)(2,1)S(1)}, bf16[72,1024]{1,0:T(8,128)(2,1)S(1)}, u32[]{:S(2)}, u32[]{:S(2)}) collective-permute-start(bf16[72,1024]{1,0:T(8,128)(2,1)S(1)} %get-tuple-element.13), channel_id=1, source_target_pairs={{32,0},{64,32},{96,64},{128,96},{160,128},{192,160},{224,192},{33,... | collective-permute-start | bytes 442376 | tf_op jit(solution)/shard_map/ppermute | solution.py:401
  3.4 0.0 copy-done.2
  3.4 5.2 %collective-permute-start = (bf16[16,512]{1,0:T(8,128)(2,1)S(1)}, bf16[16,512]{1,0:T(8,128)(2,1)S(1)}, u32[]{:S(2)}, u32[]{:S(2)}) collective-permute-start(bf16[16,512]{1,0:T(8,128)(2,1)S(1)} %copy-done.2), channel_id=1, source_target_pairs={{0,0},{1,1},{2,2},{3,3},{4,4},{5,5},{6,6},{7,7},{8,8},{9,9},{10,10... | collective-permute-start | bytes 49160 | tf_op jit(solution)/shard_map/ppermute | solution.py:409
  8.6 3.5 %collective-permute-start.1 = (bf16[72,1024]{1,0:T(8,128)(2,1)S(1)}, bf16[72,1024]{1,0:T(8,128)(2,1)S(1)}, u32[]{:S(2)}, u32[]{:S(2)}) collective-permute-start(bf16[72,1024]{1,0:T(8,128)(2,1)S(1)} %get-tuple-element.19), channel_id=1, source_target_pairs={{0,32},{32,64},{64,96},{96,128},{128,160},{160,192},{192,224},{1,3... | collective-permute-start | bytes 442376 | tf_op jit(solution)/shard_map/ppermute | solution.py:400
  12.0 0.0 copy-done
  12.0 0.0 copy-done.1
  12.1 3.0 %prepare.1 = (bf16[64,128,128]{2,1,0:T(8,128)(2,1)S(1)}, bf16[64,128,128]{2,1,0:T(8,128)(2,1)S(1)}) custom-call(bf16[16,64,1024]{2,1,0:T(8,128)(2,1)S(1)} %copy-done, bf16[64,1024]{1,0:T(8,128)(2,1)S(1)} %copy-done.1), custom_call_target="tpu_custom_call" | custom-call | flops 2147483648 | bytes 8388608 | tf_op jit(solution)/shard_map/prepare/pallas_call | solution.py:123
  15.1 0.0 collective-permute-done.refs_0_
  15.1 0.0 collective-permute-done.2.high_ref
  15.1 0.0 collective-permute-done.1.low_ref
  15.1 12.1 %chebyshev.1 = bf16[32,16,2048]{2,1,0:T(8,128)(2,1)} custom-call(bf16[64,128,128]{2,1,0:T(8,128)(2,1)S(1)} %get-tuple-element.17.field_ref, bf16[64,128,128]{2,1,0:T(8,128)(2,1)S(1)} %get-tuple-element.18.pot_ref, bf16[72,1024]{1,0:T(8,128)(2,1)S(1)} %collective-permute-done.1.low_ref, bf16[72,1024]{1,0:T(8,128)(2,1)S(1)} %collective-permute-done.2.high_ref), custom_call_target="tpu_custom_call" | custom-call | tf_op jit(solution)/shard_map/chebyshev/pallas_call | solution.py:295
  27.3 9.6 %all-to-all-start = ((bf16[32,16,2048]{2,1,0:T(8,128)(2,1)}), bf16[32,16,2048]{2,1,0:T(8,128)(2,1)S(1)}, u32[]{:S(2)}, u32[]{:S(2)}) async-start(bf16[32,16,2048]{2,1,0:T(8,128)(2,1)} %chebyshev.1), calls=%async_computation | async-start | bytes 4194304 | tf_op jit(solution)/shard_map/all_to_all | solution.py:414
  36.8 0.4 collective-permute-start.3
  37.3 0.8 collective-permute-done.3.refs_1_
  38.1 1.9 %collective-permute-start.4 = (bf16[32,512]{1,0:T(8,128)(2,1)S(1)}, bf16[32,512]{1,0:T(8,128)(2,1)S(1)}, u32[]{:S(2)}, u32[]{:S(2)}) collective-permute-start(bf16[32,512]{1,0:T(8,128)(2,1)S(1)} %pad_maximum_fusion.2), channel_id=1, source_target_pairs={{0,64},{32,96},{64,128},{96,160},{128,192},{160,224},{192,0},{224,... | collective-permute-start | bytes 98312 | tf_op jit(solution)/shard_map/ppermute | solution.py:424
  40.1 2.0 %collective-permute-done.4.refs_2_ = bf16[32,512]{1,0:T(8,128)(2,1)S(1)} collective-permute-done((bf16[32,512]{1,0:T(8,128)(2,1)S(1)}, bf16[32,512]{1,0:T(8,128)(2,1)S(1)}, u32[]{:S(2)}, u32[]{:S(2)}) %collective-permute-start.4) | collective-permute-done | bytes 32800 | tf_op jit(solution)/shard_map/ppermute | solution.py:424
  42.0 1.5 %collective-permute-start.5 = (bf16[64,512]{1,0:T(8,128)(2,1)S(1)}, bf16[64,512]{1,0:T(8,128)(2,1)S(1)}, u32[]{:S(2)}, u32[]{:S(2)}) collective-permute-start(bf16[64,512]{1,0:T(8,128)(2,1)S(1)} %pad_maximum_fusion.1), channel_id=1, source_target_pairs={{0,128},{32,160},{64,192},{96,224},{128,0},{160,32},{192,64},{224,... | collective-permute-start | bytes 196616 | tf_op jit(solution)/shard_map/ppermute | solution.py:424
  43.5 4.3 %collective-permute-done.5.refs_3_ = bf16[64,512]{1,0:T(8,128)(2,1)S(1)} collective-permute-done((bf16[64,512]{1,0:T(8,128)(2,1)S(1)}, bf16[64,512]{1,0:T(8,128)(2,1)S(1)}, u32[]{:S(2)}, u32[]{:S(2)}) %collective-permute-start.5) | collective-permute-done | bytes 65568 | tf_op jit(solution)/shard_map/ppermute | solution.py:424
  47.8 1.9 %collective-permute-start.6 = (bf16[128,512]{1,0:T(8,128)(2,1)S(1)}, bf16[128,512]{1,0:T(8,128)(2,1)S(1)}, u32[]{:S(2)}, u32[]{:S(2)}) collective-permute-start(bf16[128,512]{1,0:T(8,128)(2,1)S(1)} %pad_maximum_fusion), channel_id=1, source_target_pairs={{0,8},{1,9},{2,10},{3,11},{4,12},{5,13},{6,14},{7,15},{8,16},{9,17... | collective-permute-start | bytes 393224 | tf_op jit(solution)/shard_map/ppermute | solution.py:424
  49.7 6.8 %collective-permute-done.6.refs_4_ = bf16[128,512]{1,0:T(8,128)(2,1)S(1)} collective-permute-done((bf16[128,512]{1,0:T(8,128)(2,1)S(1)}, bf16[128,512]{1,0:T(8,128)(2,1)S(1)}, u32[]{:S(2)}, u32[]{:S(2)}) %collective-permute-start.6) | collective-permute-done | bytes 131104 | tf_op jit(solution)/shard_map/ppermute | solution.py:424
  56.5 1.0 %collective-permute-start.7 = (bf16[256,512]{1,0:T(8,128)(2,1)S(1)}, bf16[256,512]{1,0:T(8,128)(2,1)S(1)}, u32[]{:S(2)}, u32[]{:S(2)}) collective-permute-start(bf16[256,512]{1,0:T(8,128)(2,1)S(1)} %constant_dynamic-update-slice_fusion), channel_id=1, source_target_pairs={{0,16},{1,17},{2,18},{3,19},{4,20},{5,21},{6,22},{7,23},{8,24},{9,... | collective-permute-start | bytes 786440 | tf_op jit(solution)/shard_map/ppermute | solution.py:424
  57.4 0.1 stack.15.place_ref
  57.5 14.8 %collective-permute-done.7.refs_5_ = bf16[256,512]{1,0:T(8,128)(2,1)S(1)} collective-permute-done((bf16[256,512]{1,0:T(8,128)(2,1)S(1)}, bf16[256,512]{1,0:T(8,128)(2,1)S(1)}, u32[]{:S(2)}, u32[]{:S(2)}) %collective-permute-start.7) | collective-permute-done | bytes 262176 | tf_op jit(solution)/shard_map/ppermute | solution.py:424
  72.3 1.0 %order.1.r_ref = bf16[512,512]{1,0:T(8,128)(2,1)S(1)} custom-call(s32[5]{0:T(128)S(1)} %stack.15.place_ref, bf16[16,512]{1,0:T(8,128)(2,1)S(1)} %collective-permute-done.refs_0_, bf16[16,512]{1,0:T(8,128)(2,1)S(1)} %collective-permute-done.3.refs_1_, bf16[32,512]{1,0:T(8,128)(2,1)S(1)} %collective-permute-done.4.refs_2_, ...), custom_call_target="tpu_custom_call" | custom-call | tf_op jit(solution)/shard_map/order/pallas_call | solution.py:378
  73.3 14.2 %all-to-all-done = bf16[32,16,2048]{2,1,0:T(8,128)(2,1)S(1)} async-done(((bf16[32,16,2048]{2,1,0:T(8,128)(2,1)}), bf16[32,16,2048]{2,1,0:T(8,128)(2,1)S(1)}, u32[]{:S(2)}, u32[]{:S(2)}) %all-to-all-start) | async-done | bytes 2097184 | tf_op jit(solution)/shard_map/all_to_all | solution.py:414
  87.5 2.2 %rotate.1 = bf16[512,2048]{1,0:T(8,128)(2,1)} custom-call(bf16[512,512]{1,0:T(8,128)(2,1)S(1)} %order.1.r_ref, bf16[512,2048]{1,0:T(8,128)(2,1)S(1)} %bitcast.4), custom_call_target="tpu_custom_call" | custom-call | tf_op jit(solution)/shard_map/rotate/pallas_call | solution.py:339
  (8 shorter events, 0.0 us)
Async XLA Ops:
  0.0 12.0 %copy-start = (bf16[16,64,1024]{2,1,0:T(8,128)(2,1)S(1)}, bf16[16,64,1024]{2,1,0:T(8,128)(2,1)}, u32[]{:S(2)}) copy-start(bf16[16,64,1024]{2,1,0:T(8,128)(2,1)} %x_ref.1) | copy-start | bytes 6291460
  0.0 12.0 %copy-start.1 = (bf16[64,1024]{1,0:T(8,128)(2,1)S(1)}, bf16[64,1024]{1,0:T(8,128)(2,1)}, u32[]{:S(2)}) copy-start(bf16[64,1024]{1,0:T(8,128)(2,1)} %pot_ref.1) | copy-start | bytes 393220
  0.0 3.4 %copy-start.2 = (bf16[16,512]{1,0:T(8,128)(2,1)S(1)}, bf16[16,512]{1,0:T(8,128)(2,1)}, u32[]{:S(2)}) copy-start(bf16[16,512]{1,0:T(8,128)(2,1)} %param.5) | copy-start | bytes 49156
  1.4 13.7 %collective-permute-start.2 = (bf16[72,1024]{1,0:T(8,128)(2,1)S(1)}, bf16[72,1024]{1,0:T(8,128)(2,1)S(1)}, u32[]{:S(2)}, u32[]{:S(2)}) collective-permute-start(bf16[72,1024]{1,0:T(8,128)(2,1)S(1)} %get-tuple-element.13), channel_id=1, source_target_pairs={{32,0},{64,32},{96,64},{128,96},{160,128},{192,160},{224,192},{33,... | collective-permute-start | bytes 442376 | tf_op jit(solution)/shard_map/ppermute | solution.py:401
  3.4 11.7 %collective-permute-start = (bf16[16,512]{1,0:T(8,128)(2,1)S(1)}, bf16[16,512]{1,0:T(8,128)(2,1)S(1)}, u32[]{:S(2)}, u32[]{:S(2)}) collective-permute-start(bf16[16,512]{1,0:T(8,128)(2,1)S(1)} %copy-done.2), channel_id=1, source_target_pairs={{0,0},{1,1},{2,2},{3,3},{4,4},{5,5},{6,6},{7,7},{8,8},{9,9},{10,10... | collective-permute-start | bytes 49160 | tf_op jit(solution)/shard_map/ppermute | solution.py:409
  8.6 6.6 %collective-permute-start.1 = (bf16[72,1024]{1,0:T(8,128)(2,1)S(1)}, bf16[72,1024]{1,0:T(8,128)(2,1)S(1)}, u32[]{:S(2)}, u32[]{:S(2)}) collective-permute-start(bf16[72,1024]{1,0:T(8,128)(2,1)S(1)} %get-tuple-element.19), channel_id=1, source_target_pairs={{0,32},{32,64},{64,96},{96,128},{128,160},{160,192},{192,224},{1,3... | collective-permute-start | bytes 442376 | tf_op jit(solution)/shard_map/ppermute | solution.py:400
  27.3 60.2 %all-to-all-start = ((bf16[32,16,2048]{2,1,0:T(8,128)(2,1)}), bf16[32,16,2048]{2,1,0:T(8,128)(2,1)S(1)}, u32[]{:S(2)}, u32[]{:S(2)}) async-start(bf16[32,16,2048]{2,1,0:T(8,128)(2,1)} %chebyshev.1), calls=%async_computation | async-start | bytes 4194304 | tf_op jit(solution)/shard_map/all_to_all | solution.py:414
  36.8 1.3 %collective-permute-start.3 = (bf16[16,512]{1,0:T(8,128)(2,1)S(1)}, bf16[16,512]{1,0:T(8,128)(2,1)S(1)}, u32[]{:S(2)}, u32[]{:S(2)}) collective-permute-start(bf16[16,512]{1,0:T(8,128)(2,1)S(1)} %collective-permute-done.refs_0_), channel_id=1, source_target_pairs={{0,32},{32,0},{64,96},{96,64},{128,160},{160,128},{192,224},{224,1... | collective-permute-start | bytes 49160 | tf_op jit(solution)/shard_map/ppermute | solution.py:424
  38.1 3.9 %collective-permute-start.4 = (bf16[32,512]{1,0:T(8,128)(2,1)S(1)}, bf16[32,512]{1,0:T(8,128)(2,1)S(1)}, u32[]{:S(2)}, u32[]{:S(2)}) collective-permute-start(bf16[32,512]{1,0:T(8,128)(2,1)S(1)} %pad_maximum_fusion.2), channel_id=1, source_target_pairs={{0,64},{32,96},{64,128},{96,160},{128,192},{160,224},{192,0},{224,... | collective-permute-start | bytes 98312 | tf_op jit(solution)/shard_map/ppermute | solution.py:424
  42.0 5.8 %collective-permute-start.5 = (bf16[64,512]{1,0:T(8,128)(2,1)S(1)}, bf16[64,512]{1,0:T(8,128)(2,1)S(1)}, u32[]{:S(2)}, u32[]{:S(2)}) collective-permute-start(bf16[64,512]{1,0:T(8,128)(2,1)S(1)} %pad_maximum_fusion.1), channel_id=1, source_target_pairs={{0,128},{32,160},{64,192},{96,224},{128,0},{160,32},{192,64},{224,... | collective-permute-start | bytes 196616 | tf_op jit(solution)/shard_map/ppermute | solution.py:424
  47.8 8.6 %collective-permute-start.6 = (bf16[128,512]{1,0:T(8,128)(2,1)S(1)}, bf16[128,512]{1,0:T(8,128)(2,1)S(1)}, u32[]{:S(2)}, u32[]{:S(2)}) collective-permute-start(bf16[128,512]{1,0:T(8,128)(2,1)S(1)} %pad_maximum_fusion), channel_id=1, source_target_pairs={{0,8},{1,9},{2,10},{3,11},{4,12},{5,13},{6,14},{7,15},{8,16},{9,17... | collective-permute-start | bytes 393224 | tf_op jit(solution)/shard_map/ppermute | solution.py:424
  56.5 15.8 %collective-permute-start.7 = (bf16[256,512]{1,0:T(8,128)(2,1)S(1)}, bf16[256,512]{1,0:T(8,128)(2,1)S(1)}, u32[]{:S(2)}, u32[]{:S(2)}) collective-permute-start(bf16[256,512]{1,0:T(8,128)(2,1)S(1)} %constant_dynamic-update-slice_fusion), channel_id=1, source_target_pairs={{0,16},{1,17},{2,18},{3,19},{4,20},{5,21},{6,22},{7,23},{8,24},{9,... | collective-permute-start | bytes 786440 | tf_op jit(solution)/shard_map/ppermute | solution.py:424

commit v4 on v3

--- a/solution.py
+++ b/solution.py
@@ -147,7 +147,6 @@
     width = LANES * (LANES // states)
     halo = DEGREE
     b = 1.0 / cheb_scale
-    runs = [(r, q) for r in range(INNER_Y) for q in range(NZ // 8)]
 
     me, doms = lax.axis_index("dom"), lax.axis_size("dom")
     flags = (jnp.where(me > 0, 1.0, 0.0), jnp.where(me < doms - 1, 1.0, 0.0))
@@ -193,56 +192,71 @@
     first_y = lane < states
     last_y = lane >= LANES - states
 
-    def step(k, plane):
+    def sweep(k, first, count, together, emit):
         src, dst = (even, odd) if k % 2 == 1 else (odd, even)
-        base = pl.multiple_of(plane * PLANE, 8)
-
-        def rows_at(offset, r, q):
-            return src[pl.ds(base + (offset + r * RUN + 8 + q * 8), 8), :]
-
-        here = {rq: rows_at(0, *rq) for rq in runs}
-        results = {}
-        for r, q in runs:
-            v = here[r, q]
-            if r > 0:
-                below = here[r - 1, q]
-            else:
-                below = jnp.where(first_y, 0.0, pltpu.roll(here[INNER_Y - 1, q], states, 1))
-            if r < INNER_Y - 1:
-                above = here[r + 1, q]
-            else:
-                above = jnp.where(last_y, 0.0, pltpu.roll(here[0, q], LANES - states, 1))
-            along_z = rows_at(-1, r, q) + rows_at(1, r, q)
-            along_x = rows_at(-PLANE, r, q) + rows_at(PLANE, r, q)
-            a = coef[plane, r * NZ + q * 8 : r * NZ + q * 8 + 8, :]
-            t = a * v - ((below + above) + (along_z + along_x))
-            if k == 1:
-                results[r, q] = (0.5 * b) * t
-            else:
-                results[r, q] = b * t - dst[pl.ds(base + (r * RUN + 8 + q * 8), 8), :]
-        return results
-
-    def store(k, plane, results):
+        base = pl.multiple_of(first * PLANE, 8)
+        for start in range(0, NZ // 8, together):
+            cols = range(start, start + together)
+
+            def rows_at(n, r, q, offset=0):
+                return src[pl.ds(base + (n * PLANE + r * RUN + 8 + q * 8 + offset), 8), :]
+
+            def column(n):
+                return {(r, q): rows_at(n, r, q) for q in cols for r in range(INNER_Y)}
+
+            before, here = column(-1), column(0)
+            for n in range(count):
+                after = column(n + 1)
+                for r in range(INNER_Y):
+                    values = []
+                    for q in cols:
+                        v = here[r, q]
+                        if r > 0:
+                            below = here[r - 1, q]
+                        else:
+                            below = pltpu.roll(here[INNER_Y - 1, q], states, 1)
+                            below = jnp.where(first_y, 0.0, below)
+                        if r < INNER_Y - 1:
+                            above = here[r + 1, q]
+                        else:
+                            above = pltpu.roll(here[0, q], LANES - states, 1)
+                            above = jnp.where(last_y, 0.0, above)
+                        along_z = rows_at(n, r, q, -1) + rows_at(n, r, q, 1)
+                        along_x = before[r, q] + after[r, q]
+                        at = r * NZ + q * 8
+                        t = coef[first + n, at : at + 8, :] * v
+                        t = t - ((below + above) + (along_z + along_x))
+                        if k == 1:
+                            values.append((0.5 * b) * t)
+                        else:
+                            at = base + (n * PLANE + r * RUN + 8 + q * 8)
+                            values.append(b * t - dst[pl.ds(at, 8), :])
+                    emit(n, r, start, values)
+                before, here = here, after
+
+    def store(k, first, flag=None):
         dst = odd if k % 2 == 1 else even
-        base = pl.multiple_of(plane * PLANE, 8)
-        for r, q in runs:
-            dst[pl.ds(base + (r * RUN + 8 + q * 8), 8), :] = results[r, q]
+        base = pl.multiple_of(first * PLANE, 8)
+
+        def emit(n, r, q, values):
+            for i, v in enumerate(values):
+                at = base + (n * PLANE + r * RUN + 8 + (q + i) * 8)
+                dst[pl.ds(at, 8), :] = v if flag is None else v * flag
+
+        return emit
 
     unroll = 8
     for k in range(1, DEGREE):
         def outer(i, carry, k=k):
-            both = (k + i, halo + planes + i)
-            results = [step(k, plane) for plane in both]
-            for plane, flag, res in zip(both, flags, results):
-                store(k, plane, {rq: v * flag for rq, v in res.items()})
+            for plane, flag in zip((k + i, halo + planes + i), flags):
+                sweep(k, plane, 1, 1, store(k, plane, flag))
             return carry
 
         lax.fori_loop(0, halo - k, outer, 0)
 
         def body(i, carry, k=k):
-            results = [step(k, halo + unroll * i + r) for r in range(unroll)]
-            for r in range(unroll):
-                store(k, halo + unroll * i + r, results[r])
+            first = halo + unroll * i
+            sweep(k, first, unroll, 1, store(k, first))
             return carry
 
         lax.fori_loop(0, planes // unroll, body, 0)
@@ -266,11 +280,11 @@
                     ] = out[j * states : (j + 1) * states, r * LANES : (r + 1) * LANES]
 
     def last(i):
-        for r in range(unroll):
-            res = step(DEGREE, halo + unroll * i + r)
-            values = jnp.concatenate([res[rq].astype(BF16) for rq in runs], axis=0)
-            at = pl.multiple_of((unroll * i + r) * LANES, LANES)
-            done_ref[pl.ds(at, LANES), :] = values
+        def emit(n, r, q, values):
+            at = pl.multiple_of((unroll * i + n) * LANES + r * NZ + q * 8, 16)
+            done_ref[pl.ds(at, 16), :] = jnp.concatenate(values, axis=0).astype(BF16)
+
+        sweep(DEGREE, halo + unroll * i, unroll, 2, emit)
 
     def both(i, carry):
         finish(i - 1)
@@ -361,9 +375,9 @@
     def bit(n):
         return (r >> n) & 1
 
-    source = ((dom + 2 * doms - 4 * bit(2) - 2 * bit(1)) & (doms - 1)) ^ bit(0)
+    source = ((dom + 2 * doms - 4 * bit(4) - 2 * bit(3)) & (doms - 1)) ^ bit(2)
     zs = (z + doms - source) & (doms - 1)
-    y_source = (y + 2 * ys - bit(3) - 2 * bit(4)) & (ys - 1)
+    y_source = (y + 2 * ys - bit(0) - 2 * bit(1)) & (ys - 1)
     want = (y_source * doms + zs) * own
     want = want + lax.broadcasted_iota(jnp.int32, (8, total), 1) % own
     rows = lax.broadcasted_iota(jnp.int32, (total, total), 0)
@@ -415,11 +429,11 @@
     parts = [rows]
     swap = [(i, i ^ 1) for i in range(doms)]
     for perm, axis in (
+        ([(i, (i + zs) % owners) for i in range(owners)], "st"),
+        ([(i, (i + 2 * zs) % owners) for i in range(owners)], "st"),
         (swap, "dom"),
         ([(i, (i + 2) % doms) for i in range(doms)], "dom"),
         ([(i, (i + 4) % doms) for i in range(doms)], "dom"),
-        ([(i, (i + zs) % owners) for i in range(owners)], "st"),
-        ([(i, (i + 2 * zs) % owners) for i in range(owners)], "st"),
     ):
         parts.append(lax.ppermute(parts[0] if len(parts) == 1 else jnp.concatenate(parts), axis, perm))
     place = jnp.stack([me, spot // zs, spot % zs, jnp.int32(doms), jnp.int32(ys)])

time: 89.9 us -> 89.1 us (level)
    ppermute x5, waiting for transfers between devices: 28.6 us -> 21.2 us  [local(): lax.ppermute(parts[0] if len(parts) == 1 else jnp.concatenate(parts), axi...]
    all_to_all x1, waiting for transfers between devices: 14.2 us -> 21.3 us  [local(): lax.all_to_all(filtered, 'st', split_axis=0, concat_axis=0, tiled=True)]
where the time goes in v4:
time: 89.1 us; the launch traced here: 88.8 us
  waiting for transfers between devices  42.5 us (48%)
  starting transfers between devices  27.2 us (31%)
  Pallas kernels  18.9 us (21%)
    all_to_all x1, waiting for transfers between devices, local(): lax.all_to_all(filtered, 'st', split_axis=0, concat_axis=0, tiled=True)  21.3 us
    ppermute x5, waiting for transfers between devices, local(): lax.ppermute(parts[0] if len(parts) == 1 else jnp.concatenate(parts), axi...  21.2 us
    pallas_call x1, Pallas kernels, chebyshev(): pl.pallas_call(filter_kernel, in_specs=[pl.BlockSpec(memory_space=pltpu.V...  11.3 us
    all_to_all x1, starting transfers between devices, local(): lax.all_to_all(filtered, 'st', split_axis=0, concat_axis=0, tiled=True)  9.57 us
    ppermute x5, starting transfers between devices, local(): lax.ppermute(parts[0] if len(parts) == 1 else jnp.concatenate(parts), axi...  7.02 us
    ppermute x1, starting transfers between devices, local(): rows = lax.ppermute(rotation, ('dom', 'st'), shift)  5.18 us
    ppermute x1, starting transfers between devices, local(): low = lax.ppermute(high_send, 'dom', up)  3.48 us
    pallas_call x1, Pallas kernels, prepare(): pl.pallas_call(prepare_kernel, grid=(planes // group,), in_specs=[pl.Bloc...  3.02 us
  transfers between devices with their start and end apart: 9, of which 6 were waited for; matrix products, arithmetic and copies ran while one was open for 0% of the time, Pallas kernels for 4%

profile of v4, /device:TPU:2, one launch (start us, length us, event | category | flops | bytes accessed | tf_op | source)
XLA Modules:
  0.0 88.8 jit_solution(16235661284319825197)
XLA Ops:
  0.0 0.0 copy-start
  0.0 0.0 copy-start.1
  0.0 0.0 copy-start.2
  0.0 1.4 %edges.1 = (bf16[72,1024]{1,0:T(8,128)(2,1)S(1)}, bf16[72,1024]{1,0:T(8,128)(2,1)S(1)}) custom-call(bf16[16,64,1024]{2,1,0:T(8,128)(2,1)} %x_ref.1, bf16[16,64,1024]{2,1,0:T(8,128)(2,1)} %x_ref.1, bf16[64,1024]{1,0:T(8,128)(2,1)} %pot_ref.1, bf16[64,1024]{1,0:T(8,128)(2,1)} %pot_ref.1), custom_call_target="tpu_custom_call" | custom-call | tf_op jit(solution)/shard_map/edges/pallas_call | solution.py:68
  1.4 1.9 %collective-permute-start.2 = (bf16[72,1024]{1,0:T(8,128)(2,1)S(1)}, bf16[72,1024]{1,0:T(8,128)(2,1)S(1)}, u32[]{:S(2)}, u32[]{:S(2)}) collective-permute-start(bf16[72,1024]{1,0:T(8,128)(2,1)S(1)} %get-tuple-element.13), channel_id=1, source_target_pairs={{32,0},{64,32},{96,64},{128,96},{160,128},{192,160},{224,192},{33,... | collective-permute-start | bytes 442376 | tf_op jit(solution)/shard_map/ppermute | solution.py:415
  3.4 0.0 copy-done.2
  3.4 5.2 %collective-permute-start = (bf16[16,512]{1,0:T(8,128)(2,1)S(1)}, bf16[16,512]{1,0:T(8,128)(2,1)S(1)}, u32[]{:S(2)}, u32[]{:S(2)}) collective-permute-start(bf16[16,512]{1,0:T(8,128)(2,1)S(1)} %copy-done.2), channel_id=1, source_target_pairs={{0,0},{1,1},{2,2},{3,3},{4,4},{5,5},{6,6},{7,7},{8,8},{9,9},{10,10... | collective-permute-start | bytes 49160 | tf_op jit(solution)/shard_map/ppermute | solution.py:423
  8.6 3.5 %collective-permute-start.1 = (bf16[72,1024]{1,0:T(8,128)(2,1)S(1)}, bf16[72,1024]{1,0:T(8,128)(2,1)S(1)}, u32[]{:S(2)}, u32[]{:S(2)}) collective-permute-start(bf16[72,1024]{1,0:T(8,128)(2,1)S(1)} %get-tuple-element.19), channel_id=1, source_target_pairs={{0,32},{32,64},{64,96},{96,128},{128,160},{160,192},{192,224},{1,3... | collective-permute-start | bytes 442376 | tf_op jit(solution)/shard_map/ppermute | solution.py:414
  12.0 0.0 copy-done
  12.0 0.0 copy-done.1
  12.1 3.0 %prepare.1 = (bf16[64,128,128]{2,1,0:T(8,128)(2,1)S(1)}, bf16[64,128,128]{2,1,0:T(8,128)(2,1)S(1)}) custom-call(bf16[16,64,1024]{2,1,0:T(8,128)(2,1)S(1)} %copy-done, bf16[64,1024]{1,0:T(8,128)(2,1)S(1)} %copy-done.1), custom_call_target="tpu_custom_call" | custom-call | flops 2147483648 | bytes 8388608 | tf_op jit(solution)/shard_map/prepare/pallas_call | solution.py:123
  15.1 0.0 collective-permute-done.refs_0_
  15.1 0.0 collective-permute-done.2.high_ref
  15.1 0.0 collective-permute-done.1.low_ref
  15.1 11.3 %chebyshev.1 = bf16[32,16,2048]{2,1,0:T(8,128)(2,1)} custom-call(bf16[64,128,128]{2,1,0:T(8,128)(2,1)S(1)} %get-tuple-element.17.field_ref, bf16[64,128,128]{2,1,0:T(8,128)(2,1)S(1)} %get-tuple-element.18.pot_ref, bf16[72,1024]{1,0:T(8,128)(2,1)S(1)} %collective-permute-done.1.low_ref, bf16[72,1024]{1,0:T(8,128)(2,1)S(1)} %collective-permute-done.2.high_ref), custom_call_target="tpu_custom_call" | custom-call | tf_op jit(solution)/shard_map/chebyshev/pallas_call | solution.py:309
  26.4 9.6 %all-to-all-start = ((bf16[32,16,2048]{2,1,0:T(8,128)(2,1)}), bf16[32,16,2048]{2,1,0:T(8,128)(2,1)S(1)}, u32[]{:S(2)}, u32[]{:S(2)}) async-start(bf16[32,16,2048]{2,1,0:T(8,128)(2,1)} %chebyshev.1), calls=%async_computation | async-start | bytes 4194304 | tf_op jit(solution)/shard_map/all_to_all | solution.py:428
  36.0 1.9 %collective-permute-start.3 = (bf16[16,512]{1,0:T(8,128)(2,1)S(1)}, bf16[16,512]{1,0:T(8,128)(2,1)S(1)}, u32[]{:S(2)}, u32[]{:S(2)}) collective-permute-start(bf16[16,512]{1,0:T(8,128)(2,1)S(1)} %collective-permute-done.refs_0_), channel_id=1, source_target_pairs={{0,8},{1,9},{2,10},{3,11},{4,12},{5,13},{6,14},{7,15},{8,16},{9,17... | collective-permute-start | bytes 49160 | tf_op jit(solution)/shard_map/ppermute | solution.py:438
  37.9 4.7 %collective-permute-done.3.refs_1_ = bf16[16,512]{1,0:T(8,128)(2,1)S(1)} collective-permute-done((bf16[16,512]{1,0:T(8,128)(2,1)S(1)}, bf16[16,512]{1,0:T(8,128)(2,1)S(1)}, u32[]{:S(2)}, u32[]{:S(2)}) %collective-permute-start.3) | collective-permute-done | bytes 16416 | tf_op jit(solution)/shard_map/ppermute | solution.py:438
  42.6 1.7 %collective-permute-start.4 = (bf16[32,512]{1,0:T(8,128)(2,1)S(1)}, bf16[32,512]{1,0:T(8,128)(2,1)S(1)}, u32[]{:S(2)}, u32[]{:S(2)}) collective-permute-start(bf16[32,512]{1,0:T(8,128)(2,1)S(1)} %pad_maximum_fusion.2), channel_id=1, source_target_pairs={{0,16},{1,17},{2,18},{3,19},{4,20},{5,21},{6,22},{7,23},{8,24},{9,... | collective-permute-start | bytes 98312 | tf_op jit(solution)/shard_map/ppermute | solution.py:438
  44.2 4.1 %collective-permute-done.4.refs_2_ = bf16[32,512]{1,0:T(8,128)(2,1)S(1)} collective-permute-done((bf16[32,512]{1,0:T(8,128)(2,1)S(1)}, bf16[32,512]{1,0:T(8,128)(2,1)S(1)}, u32[]{:S(2)}, u32[]{:S(2)}) %collective-permute-start.4) | collective-permute-done | bytes 32800 | tf_op jit(solution)/shard_map/ppermute | solution.py:438
  48.3 0.0 collective-permute-start.5
  48.4 1.2 %collective-permute-done.5.refs_3_ = bf16[64,512]{1,0:T(8,128)(2,1)S(1)} collective-permute-done((bf16[64,512]{1,0:T(8,128)(2,1)S(1)}, bf16[64,512]{1,0:T(8,128)(2,1)S(1)}, u32[]{:S(2)}, u32[]{:S(2)}) %collective-permute-start.5) | collective-permute-done | bytes 65568 | tf_op jit(solution)/shard_map/ppermute | solution.py:438
  49.6 1.9 %collective-permute-start.6 = (bf16[128,512]{1,0:T(8,128)(2,1)S(1)}, bf16[128,512]{1,0:T(8,128)(2,1)S(1)}, u32[]{:S(2)}, u32[]{:S(2)}) collective-permute-start(bf16[128,512]{1,0:T(8,128)(2,1)S(1)} %pad_maximum_fusion), channel_id=1, source_target_pairs={{0,64},{32,96},{64,128},{96,160},{128,192},{160,224},{192,0},{224,... | collective-permute-start | bytes 393224 | tf_op jit(solution)/shard_map/ppermute | solution.py:438
  51.5 3.8 %collective-permute-done.6.refs_4_ = bf16[128,512]{1,0:T(8,128)(2,1)S(1)} collective-permute-done((bf16[128,512]{1,0:T(8,128)(2,1)S(1)}, bf16[128,512]{1,0:T(8,128)(2,1)S(1)}, u32[]{:S(2)}, u32[]{:S(2)}) %collective-permute-start.6) | collective-permute-done | bytes 131104 | tf_op jit(solution)/shard_map/ppermute | solution.py:438
  55.3 1.6 %collective-permute-start.7 = (bf16[256,512]{1,0:T(8,128)(2,1)S(1)}, bf16[256,512]{1,0:T(8,128)(2,1)S(1)}, u32[]{:S(2)}, u32[]{:S(2)}) collective-permute-start(bf16[256,512]{1,0:T(8,128)(2,1)S(1)} %constant_dynamic-update-slice_fusion), channel_id=1, source_target_pairs={{0,128},{32,160},{64,192},{96,224},{128,0},{160,32},{192,64},{224,... | collective-permute-start | bytes 786440 | tf_op jit(solution)/shard_map/ppermute | solution.py:438
  56.9 0.1 stack.15.place_ref
  56.9 7.4 %collective-permute-done.7.refs_5_ = bf16[256,512]{1,0:T(8,128)(2,1)S(1)} collective-permute-done((bf16[256,512]{1,0:T(8,128)(2,1)S(1)}, bf16[256,512]{1,0:T(8,128)(2,1)S(1)}, u32[]{:S(2)}, u32[]{:S(2)}) %collective-permute-start.7) | collective-permute-done | bytes 262176 | tf_op jit(solution)/shard_map/ppermute | solution.py:438
  64.4 1.0 %order.1.r_ref = bf16[512,512]{1,0:T(8,128)(2,1)S(1)} custom-call(s32[5]{0:T(128)S(1)} %stack.15.place_ref, bf16[16,512]{1,0:T(8,128)(2,1)S(1)} %collective-permute-done.refs_0_, bf16[16,512]{1,0:T(8,128)(2,1)S(1)} %collective-permute-done.3.refs_1_, bf16[32,512]{1,0:T(8,128)(2,1)S(1)} %collective-permute-done.4.refs_2_, ...), custom_call_target="tpu_custom_call" | custom-call | tf_op jit(solution)/shard_map/order/pallas_call | solution.py:392
  65.3 21.3 %all-to-all-done = bf16[32,16,2048]{2,1,0:T(8,128)(2,1)S(1)} async-done(((bf16[32,16,2048]{2,1,0:T(8,128)(2,1)}), bf16[32,16,2048]{2,1,0:T(8,128)(2,1)S(1)}, u32[]{:S(2)}, u32[]{:S(2)}) %all-to-all-start) | async-done | bytes 2097184 | tf_op jit(solution)/shard_map/all_to_all | solution.py:428
  86.6 2.2 %rotate.1 = bf16[512,2048]{1,0:T(8,128)(2,1)} custom-call(bf16[512,512]{1,0:T(8,128)(2,1)S(1)} %order.1.r_ref, bf16[512,2048]{1,0:T(8,128)(2,1)S(1)} %bitcast.4), custom_call_target="tpu_custom_call" | custom-call | tf_op jit(solution)/shard_map/rotate/pallas_call | solution.py:353
  (8 shorter events, 0.0 us)
Async XLA Ops:
  0.0 12.0 %copy-start = (bf16[16,64,1024]{2,1,0:T(8,128)(2,1)S(1)}, bf16[16,64,1024]{2,1,0:T(8,128)(2,1)}, u32[]{:S(2)}) copy-start(bf16[16,64,1024]{2,1,0:T(8,128)(2,1)} %x_ref.1) | copy-start | bytes 6291460
  0.0 12.0 %copy-start.1 = (bf16[64,1024]{1,0:T(8,128)(2,1)S(1)}, bf16[64,1024]{1,0:T(8,128)(2,1)}, u32[]{:S(2)}) copy-start(bf16[64,1024]{1,0:T(8,128)(2,1)} %pot_ref.1) | copy-start | bytes 393220
  0.0 3.4 %copy-start.2 = (bf16[16,512]{1,0:T(8,128)(2,1)S(1)}, bf16[16,512]{1,0:T(8,128)(2,1)}, u32[]{:S(2)}) copy-start(bf16[16,512]{1,0:T(8,128)(2,1)} %param.5) | copy-start | bytes 49156
  1.4 13.7 %collective-permute-start.2 = (bf16[72,1024]{1,0:T(8,128)(2,1)S(1)}, bf16[72,1024]{1,0:T(8,128)(2,1)S(1)}, u32[]{:S(2)}, u32[]{:S(2)}) collective-permute-start(bf16[72,1024]{1,0:T(8,128)(2,1)S(1)} %get-tuple-element.13), channel_id=1, source_target_pairs={{32,0},{64,32},{96,64},{128,96},{160,128},{192,160},{224,192},{33,... | collective-permute-start | bytes 442376 | tf_op jit(solution)/shard_map/ppermute | solution.py:415
  3.4 11.7 %collective-permute-start = (bf16[16,512]{1,0:T(8,128)(2,1)S(1)}, bf16[16,512]{1,0:T(8,128)(2,1)S(1)}, u32[]{:S(2)}, u32[]{:S(2)}) collective-permute-start(bf16[16,512]{1,0:T(8,128)(2,1)S(1)} %copy-done.2), channel_id=1, source_target_pairs={{0,0},{1,1},{2,2},{3,3},{4,4},{5,5},{6,6},{7,7},{8,8},{9,9},{10,10... | collective-permute-start | bytes 49160 | tf_op jit(solution)/shard_map/ppermute | solution.py:423
  8.6 6.6 %collective-permute-start.1 = (bf16[72,1024]{1,0:T(8,128)(2,1)S(1)}, bf16[72,1024]{1,0:T(8,128)(2,1)S(1)}, u32[]{:S(2)}, u32[]{:S(2)}) collective-permute-start(bf16[72,1024]{1,0:T(8,128)(2,1)S(1)} %get-tuple-element.19), channel_id=1, source_target_pairs={{0,32},{32,64},{64,96},{96,128},{128,160},{160,192},{192,224},{1,3... | collective-permute-start | bytes 442376 | tf_op jit(solution)/shard_map/ppermute | solution.py:414
  26.4 60.2 %all-to-all-start = ((bf16[32,16,2048]{2,1,0:T(8,128)(2,1)}), bf16[32,16,2048]{2,1,0:T(8,128)(2,1)S(1)}, u32[]{:S(2)}, u32[]{:S(2)}) async-start(bf16[32,16,2048]{2,1,0:T(8,128)(2,1)} %chebyshev.1), calls=%async_computation | async-start | bytes 4194304 | tf_op jit(solution)/shard_map/all_to_all | solution.py:428
  36.0 6.5 %collective-permute-start.3 = (bf16[16,512]{1,0:T(8,128)(2,1)S(1)}, bf16[16,512]{1,0:T(8,128)(2,1)S(1)}, u32[]{:S(2)}, u32[]{:S(2)}) collective-permute-start(bf16[16,512]{1,0:T(8,128)(2,1)S(1)} %collective-permute-done.refs_0_), channel_id=1, source_target_pairs={{0,8},{1,9},{2,10},{3,11},{4,12},{5,13},{6,14},{7,15},{8,16},{9,17... | collective-permute-start | bytes 49160 | tf_op jit(solution)/shard_map/ppermute | solution.py:438
  42.6 5.8 %collective-permute-start.4 = (bf16[32,512]{1,0:T(8,128)(2,1)S(1)}, bf16[32,512]{1,0:T(8,128)(2,1)S(1)}, u32[]{:S(2)}, u32[]{:S(2)}) collective-permute-start(bf16[32,512]{1,0:T(8,128)(2,1)S(1)} %pad_maximum_fusion.2), channel_id=1, source_target_pairs={{0,16},{1,17},{2,18},{3,19},{4,20},{5,21},{6,22},{7,23},{8,24},{9,... | collective-permute-start | bytes 98312 | tf_op jit(solution)/shard_map/ppermute | solution.py:438
  48.3 1.3 %collective-permute-start.5 = (bf16[64,512]{1,0:T(8,128)(2,1)S(1)}, bf16[64,512]{1,0:T(8,128)(2,1)S(1)}, u32[]{:S(2)}, u32[]{:S(2)}) collective-permute-start(bf16[64,512]{1,0:T(8,128)(2,1)S(1)} %pad_maximum_fusion.1), channel_id=1, source_target_pairs={{0,32},{32,0},{64,96},{96,64},{128,160},{160,128},{192,224},{224,1... | collective-permute-start | bytes 196616 | tf_op jit(solution)/shard_map/ppermute | solution.py:438
  49.6 5.6 %collective-permute-start.6 = (bf16[128,512]{1,0:T(8,128)(2,1)S(1)}, bf16[128,512]{1,0:T(8,128)(2,1)S(1)}, u32[]{:S(2)}, u32[]{:S(2)}) collective-permute-start(bf16[128,512]{1,0:T(8,128)(2,1)S(1)} %pad_maximum_fusion), channel_id=1, source_target_pairs={{0,64},{32,96},{64,128},{96,160},{128,192},{160,224},{192,0},{224,... | collective-permute-start | bytes 393224 | tf_op jit(solution)/shard_map/ppermute | solution.py:438
  55.3 9.1 %collective-permute-start.7 = (bf16[256,512]{1,0:T(8,128)(2,1)S(1)}, bf16[256,512]{1,0:T(8,128)(2,1)S(1)}, u32[]{:S(2)}, u32[]{:S(2)}) collective-permute-start(bf16[256,512]{1,0:T(8,128)(2,1)S(1)} %constant_dynamic-update-slice_fusion), channel_id=1, source_target_pairs={{0,128},{32,160},{64,192},{96,224},{128,0},{160,32},{192,64},{224,... | collective-permute-start | bytes 786440 | tf_op jit(solution)/shard_map/ppermute | solution.py:438

commit v5 on v4

--- a/solution.py
+++ b/solution.py
@@ -43,6 +43,10 @@
         ],
         axis=0,
     )
+
+
+def scaled(pot):
+    return (pot - (cheb_shift - 3.0)) * 2.0
 
 
 def edges_kernel(first_ref, last_ref, pot_first_ref, pot_last_ref, low_ref, high_ref):
@@ -109,7 +113,7 @@
     rows = jnp.dot(pick, rows, preferred_element_type=F32).astype(BF16)
     for p in range(0, group, 2):
         at = slice(p * LANES, (p + 2) * LANES)
-        spreads = jnp.dot(pot, select[:, at], preferred_element_type=F32).astype(BF16)
+        spreads = scaled(jnp.dot(pot, select[:, at], preferred_element_type=F32))
         both = turned(stacked(rows, states, p, 2)).astype(BF16)
         for source, target in ((both, field_ref), (spreads, pot_out_ref)):
             target[p] = source[:, :LANES]
@@ -128,7 +132,7 @@
             pl.BlockSpec((group, width), lambda i: (i, 0)),
         ],
         out_specs=[pl.BlockSpec((group, LANES, LANES), lambda i: (i, 0, 0))] * 2,
-        out_shape=[out, out],
+        out_shape=[out, jax.ShapeDtypeStruct(out.shape, F32)],
         scratch_shapes=[pltpu.VMEM((group * width // LANES, group * LANES), BF16)],
         cost_estimate=pl.CostEstimate(
             flops=4 * 2 * states * planes * width * 256, transcendentals=0, bytes_accessed=8 << 20
@@ -150,9 +154,6 @@
 
     me, doms = lax.axis_index("dom"), lax.axis_size("dom")
     flags = (jnp.where(me > 0, 1.0, 0.0), jnp.where(me < doms - 1, 1.0, 0.0))
-    def scaled(p):
-        return (p - (cheb_shift - 3.0)) * 2.0
-
     def put(buffer, plane, values):
         for r in range(INNER_Y):
             at = pl.multiple_of(plane * PLANE + r * RUN + 8, 8)
@@ -173,7 +174,7 @@
     odd[(planes + 2 * halo) * PLANE :, :] = zero
 
     rows = DEGREE * states
-    for ref, base, at in ((low_ref, 0, 4), (high_ref, halo + planes, 0)):
+    for side, ref, base, at in ((0, low_ref, 0, 4), (1, high_ref, halo + planes, 0)):
         field = ref[:rows]
         pot = spread(ref[rows:], states)
         for p in range(0, halo, 2):
@@ -181,18 +182,17 @@
             put(even, base + p, both[:, :LANES])
             put(even, base + p + 1, both[:, LANES:])
             both = scaled(turned(stacked(pot, states, at + p, 2)))
-            coef[base + p] = both[:, :LANES]
-            coef[base + p + 1] = both[:, LANES:]
+            coef[side * halo + p] = both[:, :LANES]
+            coef[side * halo + p + 1] = both[:, LANES:]
 
     for p in range(planes):
         put(even, halo + p, field_ref[p].astype(F32))
-        coef[halo + p] = scaled(pot_ref[p].astype(F32))
 
     lane = lax.broadcasted_iota(jnp.int32, (8, LANES), 1)
     first_y = lane < states
     last_y = lane >= LANES - states
 
-    def sweep(k, first, count, together, emit):
+    def sweep(k, first, count, together, factors, place, emit):
         src, dst = (even, odd) if k % 2 == 1 else (odd, even)
         base = pl.multiple_of(first * PLANE, 8)
         for start in range(0, NZ // 8, together):
@@ -224,7 +224,7 @@
                         along_z = rows_at(n, r, q, -1) + rows_at(n, r, q, 1)
                         along_x = before[r, q] + after[r, q]
                         at = r * NZ + q * 8
-                        t = coef[first + n, at : at + 8, :] * v
+                        t = factors[place + n, at : at + 8, :] * v
                         t = t - ((below + above) + (along_z + along_x))
                         if k == 1:
                             values.append((0.5 * b) * t)
@@ -248,15 +248,16 @@
     unroll = 8
     for k in range(1, DEGREE):
         def outer(i, carry, k=k):
-            for plane, flag in zip((k + i, halo + planes + i), flags):
-                sweep(k, plane, 1, 1, store(k, plane, flag))
+            low_at, high_at = k + i, halo + planes + i
+            sweep(k, low_at, 1, 1, coef, low_at, store(k, low_at, flags[0]))
+            sweep(k, high_at, 1, 1, coef, halo + i, store(k, high_at, flags[1]))
             return carry
 
         lax.fori_loop(0, halo - k, outer, 0)
 
         def body(i, carry, k=k):
             first = halo + unroll * i
-            sweep(k, first, unroll, 1, store(k, first))
+            sweep(k, first, unroll, 1, pot_ref, unroll * i, store(k, first))
             return carry
 
         lax.fori_loop(0, planes // unroll, body, 0)
@@ -284,7 +285,7 @@
             at = pl.multiple_of((unroll * i + n) * LANES + r * NZ + q * 8, 16)
             done_ref[pl.ds(at, 16), :] = jnp.concatenate(values, axis=0).astype(BF16)
 
-        sweep(DEGREE, halo + unroll * i, unroll, 2, emit)
+        sweep(DEGREE, halo + unroll * i, unroll, 2, pot_ref, unroll * i, emit)
 
     def both(i, carry):
         finish(i - 1)
@@ -305,21 +306,21 @@
     planes = field.shape[0]
     points = planes * LANES * LANES // states // owners
     total = planes + 2 * DEGREE
-    anywhere = pl.BlockSpec(memory_space=pl.ANY)
+    hbm = pl.BlockSpec(memory_space=pltpu.HBM)
     return pl.pallas_call(
         filter_kernel,
         in_specs=[pl.BlockSpec(memory_space=pltpu.VMEM)] * 4,
-        out_specs=anywhere,
+        out_specs=hbm,
         out_shape=jax.ShapeDtypeStruct((owners, states, points), BF16),
         scratch_shapes=[
             pltpu.VMEM((total * PLANE + 8, LANES), F32),
             pltpu.VMEM((total * PLANE + 8, LANES), F32),
-            pltpu.VMEM((total, LANES, LANES), F32),
+            pltpu.VMEM((2 * DEGREE, LANES, LANES), F32),
             pltpu.VMEM((planes * LANES, LANES), BF16),
             pltpu.VMEM((owners, states, points), BF16),
             pltpu.SemaphoreType.DMA((planes // 8,)),
         ],
-        compiler_params=pltpu.CompilerParams(vmem_limit_bytes=32 << 20),
+        compiler_params=pltpu.CompilerParams(vmem_limit_bytes=59_300_000),
         name="chebyshev",
     )(*in_vmem(field, pot, low, high))
 

time: 89.1 us -> 88.8 us (level)
  transfers between devices with their start and end apart: 9 -> 9, of which waited for: 6 -> 6; matrix products, arithmetic and copies ran while one was open for 0% -> 0% of each run, Pallas kernels for 4% -> 5%
where the time goes in v5:
time: 88.8 us; the launch traced here: 88.6 us
  waiting for transfers between devices  42.4 us (48%)
  starting transfers between devices  27.2 us (31%)
  Pallas kernels  18.6 us (21%)
    all_to_all x1, waiting for transfers between devices, local(): lax.all_to_all(filtered, 'st', split_axis=0, concat_axis=0, tiled=True)  21.4 us
    ppermute x5, waiting for transfers between devices, local(): lax.ppermute(parts[0] if len(parts) == 1 else jnp.concatenate(parts), axi...  21.1 us
    pallas_call x1, Pallas kernels, chebyshev(): pl.pallas_call(filter_kernel, in_specs=[pl.BlockSpec(memory_space=pltpu.V...  11 us
    all_to_all x1, starting transfers between devices, local(): lax.all_to_all(filtered, 'st', split_axis=0, concat_axis=0, tiled=True)  9.58 us
    ppermute x5, starting transfers between devices, local(): lax.ppermute(parts[0] if len(parts) == 1 else jnp.concatenate(parts), axi...  7.08 us
    ppermute x1, starting transfers between devices, local(): rows = lax.ppermute(rotation, ('dom', 'st'), shift)  5.18 us
    ppermute x1, starting transfers between devices, local(): low = lax.ppermute(high_send, 'dom', up)  3.48 us
    pallas_call x1, Pallas kernels, prepare(): pl.pallas_call(prepare_kernel, grid=(planes // group,), in_specs=[pl.Bloc...  3.02 us
  transfers between devices with their start and end apart: 9, of which 6 were waited for; matrix products, arithmetic and copies ran while one was open for 0% of the time, Pallas kernels for 5%

profile of v5, /device:TPU:2, one launch (start us, length us, event | category | flops | bytes accessed | tf_op | source)
XLA Modules:
  0.0 88.6 jit_solution(18179308316152327853)
XLA Ops:
  0.0 0.0 copy-start
  0.0 0.0 copy-start.1
  0.0 0.0 copy-start.2
  0.0 1.4 %edges.1 = (bf16[72,1024]{1,0:T(8,128)(2,1)S(1)}, bf16[72,1024]{1,0:T(8,128)(2,1)S(1)}) custom-call(bf16[16,64,1024]{2,1,0:T(8,128)(2,1)} %x_ref.1, bf16[16,64,1024]{2,1,0:T(8,128)(2,1)} %x_ref.1, bf16[64,1024]{1,0:T(8,128)(2,1)} %pot_ref.1, bf16[64,1024]{1,0:T(8,128)(2,1)} %pot_ref.1), custom_call_target="tpu_custom_call" | custom-call | tf_op jit(solution)/shard_map/edges/pallas_call | solution.py:72
  1.4 1.9 %collective-permute-start.2 = (bf16[72,1024]{1,0:T(8,128)(2,1)S(1)}, bf16[72,1024]{1,0:T(8,128)(2,1)S(1)}, u32[]{:S(2)}, u32[]{:S(2)}) collective-permute-start(bf16[72,1024]{1,0:T(8,128)(2,1)S(1)} %get-tuple-element.13), channel_id=1, source_target_pairs={{32,0},{64,32},{96,64},{128,96},{160,128},{192,160},{224,192},{33,... | collective-permute-start | bytes 442376 | tf_op jit(solution)/shard_map/ppermute | solution.py:416
  3.4 0.0 copy-done.2
  3.4 5.2 %collective-permute-start = (bf16[16,512]{1,0:T(8,128)(2,1)S(1)}, bf16[16,512]{1,0:T(8,128)(2,1)S(1)}, u32[]{:S(2)}, u32[]{:S(2)}) collective-permute-start(bf16[16,512]{1,0:T(8,128)(2,1)S(1)} %copy-done.2), channel_id=1, source_target_pairs={{0,0},{1,1},{2,2},{3,3},{4,4},{5,5},{6,6},{7,7},{8,8},{9,9},{10,10... | collective-permute-start | bytes 49160 | tf_op jit(solution)/shard_map/ppermute | solution.py:424
  8.6 3.5 %collective-permute-start.1 = (bf16[72,1024]{1,0:T(8,128)(2,1)S(1)}, bf16[72,1024]{1,0:T(8,128)(2,1)S(1)}, u32[]{:S(2)}, u32[]{:S(2)}) collective-permute-start(bf16[72,1024]{1,0:T(8,128)(2,1)S(1)} %get-tuple-element.19), channel_id=1, source_target_pairs={{0,32},{32,64},{64,96},{96,128},{128,160},{160,192},{192,224},{1,3... | collective-permute-start | bytes 442376 | tf_op jit(solution)/shard_map/ppermute | solution.py:415
  12.0 0.0 copy-done
  12.0 0.0 copy-done.1
  12.1 3.0 %prepare.1 = (bf16[64,128,128]{2,1,0:T(8,128)(2,1)S(1)}, f32[64,128,128]{2,1,0:T(8,128)S(1)}) custom-call(bf16[16,64,1024]{2,1,0:T(8,128)(2,1)S(1)} %copy-done, bf16[64,1024]{1,0:T(8,128)(2,1)S(1)} %copy-done.1), custom_call_target="tpu_custom_call" | custom-call | flops 2147483648 | bytes 8388608 | tf_op jit(solution)/shard_map/prepare/pallas_call | solution.py:127
  15.1 0.0 collective-permute-done.refs_0_
  15.1 0.0 collective-permute-done.2.high_ref
  15.1 0.0 collective-permute-done.1.low_ref
  15.1 11.0 %chebyshev.1 = bf16[32,16,2048]{2,1,0:T(8,128)(2,1)} custom-call(bf16[64,128,128]{2,1,0:T(8,128)(2,1)S(1)} %get-tuple-element.17.field_ref, f32[64,128,128]{2,1,0:T(8,128)S(1)} %get-tuple-element.18.pot_ref, bf16[72,1024]{1,0:T(8,128)(2,1)S(1)} %collective-permute-done.1.low_ref, bf16[72,1024]{1,0:T(8,128)(2,1)S(1)} %collective-permute-done.2.high_ref), custom_call_target="tpu_custom_call" | custom-call | tf_op jit(solution)/shard_map/chebyshev/pallas_call | solution.py:310
  26.2 9.6 %all-to-all-start = ((bf16[32,16,2048]{2,1,0:T(8,128)(2,1)}), bf16[32,16,2048]{2,1,0:T(8,128)(2,1)S(1)}, u32[]{:S(2)}, u32[]{:S(2)}) async-start(bf16[32,16,2048]{2,1,0:T(8,128)(2,1)} %chebyshev.1), calls=%async_computation | async-start | bytes 4194304 | tf_op jit(solution)/shard_map/all_to_all | solution.py:429
  35.7 1.9 %collective-permute-start.3 = (bf16[16,512]{1,0:T(8,128)(2,1)S(1)}, bf16[16,512]{1,0:T(8,128)(2,1)S(1)}, u32[]{:S(2)}, u32[]{:S(2)}) collective-permute-start(bf16[16,512]{1,0:T(8,128)(2,1)S(1)} %collective-permute-done.refs_0_), channel_id=1, source_target_pairs={{0,8},{1,9},{2,10},{3,11},{4,12},{5,13},{6,14},{7,15},{8,16},{9,17... | collective-permute-start | bytes 49160 | tf_op jit(solution)/shard_map/ppermute | solution.py:439
  37.6 4.7 %collective-permute-done.3.refs_1_ = bf16[16,512]{1,0:T(8,128)(2,1)S(1)} collective-permute-done((bf16[16,512]{1,0:T(8,128)(2,1)S(1)}, bf16[16,512]{1,0:T(8,128)(2,1)S(1)}, u32[]{:S(2)}, u32[]{:S(2)}) %collective-permute-start.3) | collective-permute-done | bytes 16416 | tf_op jit(solution)/shard_map/ppermute | solution.py:439
  42.3 1.7 %collective-permute-start.4 = (bf16[32,512]{1,0:T(8,128)(2,1)S(1)}, bf16[32,512]{1,0:T(8,128)(2,1)S(1)}, u32[]{:S(2)}, u32[]{:S(2)}) collective-permute-start(bf16[32,512]{1,0:T(8,128)(2,1)S(1)} %pad_maximum_fusion.2), channel_id=1, source_target_pairs={{0,16},{1,17},{2,18},{3,19},{4,20},{5,21},{6,22},{7,23},{8,24},{9,... | collective-permute-start | bytes 98312 | tf_op jit(solution)/shard_map/ppermute | solution.py:439
  44.0 4.1 %collective-permute-done.4.refs_2_ = bf16[32,512]{1,0:T(8,128)(2,1)S(1)} collective-permute-done((bf16[32,512]{1,0:T(8,128)(2,1)S(1)}, bf16[32,512]{1,0:T(8,128)(2,1)S(1)}, u32[]{:S(2)}, u32[]{:S(2)}) %collective-permute-start.4) | collective-permute-done | bytes 32800 | tf_op jit(solution)/shard_map/ppermute | solution.py:439
  48.0 0.0 collective-permute-start.5
  48.1 1.2 %collective-permute-done.5.refs_3_ = bf16[64,512]{1,0:T(8,128)(2,1)S(1)} collective-permute-done((bf16[64,512]{1,0:T(8,128)(2,1)S(1)}, bf16[64,512]{1,0:T(8,128)(2,1)S(1)}, u32[]{:S(2)}, u32[]{:S(2)}) %collective-permute-start.5) | collective-permute-done | bytes 65568 | tf_op jit(solution)/shard_map/ppermute | solution.py:439
  49.3 1.9 %collective-permute-start.6 = (bf16[128,512]{1,0:T(8,128)(2,1)S(1)}, bf16[128,512]{1,0:T(8,128)(2,1)S(1)}, u32[]{:S(2)}, u32[]{:S(2)}) collective-permute-start(bf16[128,512]{1,0:T(8,128)(2,1)S(1)} %pad_maximum_fusion), channel_id=1, source_target_pairs={{0,64},{32,96},{64,128},{96,160},{128,192},{160,224},{192,0},{224,... | collective-permute-start | bytes 393224 | tf_op jit(solution)/shard_map/ppermute | solution.py:439
  51.2 3.7 %collective-permute-done.6.refs_4_ = bf16[128,512]{1,0:T(8,128)(2,1)S(1)} collective-permute-done((bf16[128,512]{1,0:T(8,128)(2,1)S(1)}, bf16[128,512]{1,0:T(8,128)(2,1)S(1)}, u32[]{:S(2)}, u32[]{:S(2)}) %collective-permute-start.6) | collective-permute-done | bytes 131104 | tf_op jit(solution)/shard_map/ppermute | solution.py:439
  55.0 1.6 %collective-permute-start.7 = (bf16[256,512]{1,0:T(8,128)(2,1)S(1)}, bf16[256,512]{1,0:T(8,128)(2,1)S(1)}, u32[]{:S(2)}, u32[]{:S(2)}) collective-permute-start(bf16[256,512]{1,0:T(8,128)(2,1)S(1)} %constant_dynamic-update-slice_fusion), channel_id=1, source_target_pairs={{0,128},{32,160},{64,192},{96,224},{128,0},{160,32},{192,64},{224,... | collective-permute-start | bytes 786440 | tf_op jit(solution)/shard_map/ppermute | solution.py:439
  56.6 0.1 stack.15.place_ref
  56.7 7.4 %collective-permute-done.7.refs_5_ = bf16[256,512]{1,0:T(8,128)(2,1)S(1)} collective-permute-done((bf16[256,512]{1,0:T(8,128)(2,1)S(1)}, bf16[256,512]{1,0:T(8,128)(2,1)S(1)}, u32[]{:S(2)}, u32[]{:S(2)}) %collective-permute-start.7) | collective-permute-done | bytes 262176 | tf_op jit(solution)/shard_map/ppermute | solution.py:439
  64.1 1.0 %order.1.r_ref = bf16[512,512]{1,0:T(8,128)(2,1)S(1)} custom-call(s32[5]{0:T(128)S(1)} %stack.15.place_ref, bf16[16,512]{1,0:T(8,128)(2,1)S(1)} %collective-permute-done.refs_0_, bf16[16,512]{1,0:T(8,128)(2,1)S(1)} %collective-permute-done.3.refs_1_, bf16[32,512]{1,0:T(8,128)(2,1)S(1)} %collective-permute-done.4.refs_2_, ...), custom_call_target="tpu_custom_call" | custom-call | tf_op jit(solution)/shard_map/order/pallas_call | solution.py:393
  65.0 21.4 %all-to-all-done = bf16[32,16,2048]{2,1,0:T(8,128)(2,1)S(1)} async-done(((bf16[32,16,2048]{2,1,0:T(8,128)(2,1)}), bf16[32,16,2048]{2,1,0:T(8,128)(2,1)S(1)}, u32[]{:S(2)}, u32[]{:S(2)}) %all-to-all-start) | async-done | bytes 2097184 | tf_op jit(solution)/shard_map/all_to_all | solution.py:429
  86.4 2.2 %rotate.1 = bf16[512,2048]{1,0:T(8,128)(2,1)} custom-call(bf16[512,512]{1,0:T(8,128)(2,1)S(1)} %order.1.r_ref, bf16[512,2048]{1,0:T(8,128)(2,1)S(1)} %bitcast.4), custom_call_target="tpu_custom_call" | custom-call | tf_op jit(solution)/shard_map/rotate/pallas_call | solution.py:354
  (8 shorter events, 0.0 us)
Async XLA Ops:
  0.0 12.0 %copy-start = (bf16[16,64,1024]{2,1,0:T(8,128)(2,1)S(1)}, bf16[16,64,1024]{2,1,0:T(8,128)(2,1)}, u32[]{:S(2)}) copy-start(bf16[16,64,1024]{2,1,0:T(8,128)(2,1)} %x_ref.1) | copy-start | bytes 6291460
  0.0 12.0 %copy-start.1 = (bf16[64,1024]{1,0:T(8,128)(2,1)S(1)}, bf16[64,1024]{1,0:T(8,128)(2,1)}, u32[]{:S(2)}) copy-start(bf16[64,1024]{1,0:T(8,128)(2,1)} %pot_ref.1) | copy-start | bytes 393220
  0.0 3.4 %copy-start.2 = (bf16[16,512]{1,0:T(8,128)(2,1)S(1)}, bf16[16,512]{1,0:T(8,128)(2,1)}, u32[]{:S(2)}) copy-start(bf16[16,512]{1,0:T(8,128)(2,1)} %param.5) | copy-start | bytes 49156
  1.4 13.7 %collective-permute-start.2 = (bf16[72,1024]{1,0:T(8,128)(2,1)S(1)}, bf16[72,1024]{1,0:T(8,128)(2,1)S(1)}, u32[]{:S(2)}, u32[]{:S(2)}) collective-permute-start(bf16[72,1024]{1,0:T(8,128)(2,1)S(1)} %get-tuple-element.13), channel_id=1, source_target_pairs={{32,0},{64,32},{96,64},{128,96},{160,128},{192,160},{224,192},{33,... | collective-permute-start | bytes 442376 | tf_op jit(solution)/shard_map/ppermute | solution.py:416
  3.4 11.7 %collective-permute-start = (bf16[16,512]{1,0:T(8,128)(2,1)S(1)}, bf16[16,512]{1,0:T(8,128)(2,1)S(1)}, u32[]{:S(2)}, u32[]{:S(2)}) collective-permute-start(bf16[16,512]{1,0:T(8,128)(2,1)S(1)} %copy-done.2), channel_id=1, source_target_pairs={{0,0},{1,1},{2,2},{3,3},{4,4},{5,5},{6,6},{7,7},{8,8},{9,9},{10,10... | collective-permute-start | bytes 49160 | tf_op jit(solution)/shard_map/ppermute | solution.py:424
  8.6 6.6 %collective-permute-start.1 = (bf16[72,1024]{1,0:T(8,128)(2,1)S(1)}, bf16[72,1024]{1,0:T(8,128)(2,1)S(1)}, u32[]{:S(2)}, u32[]{:S(2)}) collective-permute-start(bf16[72,1024]{1,0:T(8,128)(2,1)S(1)} %get-tuple-element.19), channel_id=1, source_target_pairs={{0,32},{32,64},{64,96},{96,128},{128,160},{160,192},{192,224},{1,3... | collective-permute-start | bytes 442376 | tf_op jit(solution)/shard_map/ppermute | solution.py:415
  26.2 60.2 %all-to-all-start = ((bf16[32,16,2048]{2,1,0:T(8,128)(2,1)}), bf16[32,16,2048]{2,1,0:T(8,128)(2,1)S(1)}, u32[]{:S(2)}, u32[]{:S(2)}) async-start(bf16[32,16,2048]{2,1,0:T(8,128)(2,1)} %chebyshev.1), calls=%async_computation | async-start | bytes 4194304 | tf_op jit(solution)/shard_map/all_to_all | solution.py:429
  35.7 6.5 %collective-permute-start.3 = (bf16[16,512]{1,0:T(8,128)(2,1)S(1)}, bf16[16,512]{1,0:T(8,128)(2,1)S(1)}, u32[]{:S(2)}, u32[]{:S(2)}) collective-permute-start(bf16[16,512]{1,0:T(8,128)(2,1)S(1)} %collective-permute-done.refs_0_), channel_id=1, source_target_pairs={{0,8},{1,9},{2,10},{3,11},{4,12},{5,13},{6,14},{7,15},{8,16},{9,17... | collective-permute-start | bytes 49160 | tf_op jit(solution)/shard_map/ppermute | solution.py:439
  42.3 5.8 %collective-permute-start.4 = (bf16[32,512]{1,0:T(8,128)(2,1)S(1)}, bf16[32,512]{1,0:T(8,128)(2,1)S(1)}, u32[]{:S(2)}, u32[]{:S(2)}) collective-permute-start(bf16[32,512]{1,0:T(8,128)(2,1)S(1)} %pad_maximum_fusion.2), channel_id=1, source_target_pairs={{0,16},{1,17},{2,18},{3,19},{4,20},{5,21},{6,22},{7,23},{8,24},{9,... | collective-permute-start | bytes 98312 | tf_op jit(solution)/shard_map/ppermute | solution.py:439
  48.0 1.3 %collective-permute-start.5 = (bf16[64,512]{1,0:T(8,128)(2,1)S(1)}, bf16[64,512]{1,0:T(8,128)(2,1)S(1)}, u32[]{:S(2)}, u32[]{:S(2)}) collective-permute-start(bf16[64,512]{1,0:T(8,128)(2,1)S(1)} %pad_maximum_fusion.1), channel_id=1, source_target_pairs={{0,32},{32,0},{64,96},{96,64},{128,160},{160,128},{192,224},{224,1... | collective-permute-start | bytes 196616 | tf_op jit(solution)/shard_map/ppermute | solution.py:439
  49.3 5.6 %collective-permute-start.6 = (bf16[128,512]{1,0:T(8,128)(2,1)S(1)}, bf16[128,512]{1,0:T(8,128)(2,1)S(1)}, u32[]{:S(2)}, u32[]{:S(2)}) collective-permute-start(bf16[128,512]{1,0:T(8,128)(2,1)S(1)} %pad_maximum_fusion), channel_id=1, source_target_pairs={{0,64},{32,96},{64,128},{96,160},{128,192},{160,224},{192,0},{224,... | collective-permute-start | bytes 393224 | tf_op jit(solution)/shard_map/ppermute | solution.py:439
  55.0 9.1 %collective-permute-start.7 = (bf16[256,512]{1,0:T(8,128)(2,1)S(1)}, bf16[256,512]{1,0:T(8,128)(2,1)S(1)}, u32[]{:S(2)}, u32[]{:S(2)}) collective-permute-start(bf16[256,512]{1,0:T(8,128)(2,1)S(1)} %constant_dynamic-update-slice_fusion), channel_id=1, source_target_pairs={{0,128},{32,160},{64,192},{96,224},{128,0},{160,32},{192,64},{224,... | collective-permute-start | bytes 786440 | tf_op jit(solution)/shard_map/ppermute | solution.py:439

commit v6 on v5

--- a/solution.py
+++ b/solution.py
@@ -420,12 +420,11 @@
         for y in range(ys)
         for z in range(zs)
     ]
-    rotation, low_send = lax.optimization_barrier((rotation, low_send))
+    field, pot = prepare(orbitals, potential)
+    rotation, field = lax.optimization_barrier((rotation, field))
     rows = lax.ppermute(rotation, ("dom", "st"), shift)
-    field, pot = prepare(orbitals, potential)
-    rows, field = lax.optimization_barrier((rows, field))
     filtered = chebyshev(field, pot, low, high, owners, states)
-    rows, _ = lax.optimization_barrier((rows, filtered))
+    rows, filtered = lax.optimization_barrier((rows, filtered))
     regrouped = lax.all_to_all(filtered, "st", split_axis=0, concat_axis=0, tiled=True)
     parts = [rows]
     swap = [(i, i ^ 1) for i in range(doms)]

time: 88.8 us -> 88.8 us (level)
    ppermute x1, starting transfers between devices: 1.92 us -> 3.64 us  [local(): high = lax.ppermute(low_send, 'dom', down)]
    ppermute x1, starting transfers between devices: 3.48 us -> 1.92 us  [local(): low = lax.ppermute(high_send, 'dom', up)]
  transfers between devices with their start and end apart: 9 -> 9, of which waited for: 6 -> 6; matrix products, arithmetic and copies ran while one was open for 0% -> 0% of each run, Pallas kernels for 5% -> 17%
where the time goes in v6:
time: 88.8 us; the launch traced here: 88.5 us
  waiting for transfers between devices  42.5 us (48%)
  starting transfers between devices  27.1 us (31%)
  Pallas kernels  18.6 us (21%)
    ppermute x5, waiting for transfers between devices, local(): lax.ppermute(parts[0] if len(parts) == 1 else jnp.concatenate(parts), axi...  21.3 us
    all_to_all x1, waiting for transfers between devices, local(): lax.all_to_all(filtered, 'st', split_axis=0, concat_axis=0, tiled=True)  21.2 us
    pallas_call x1, Pallas kernels, chebyshev(): pl.pallas_call(filter_kernel, in_specs=[pl.BlockSpec(memory_space=pltpu.V...  11 us
    all_to_all x1, starting transfers between devices, local(): lax.all_to_all(filtered, 'st', split_axis=0, concat_axis=0, tiled=True)  9.7 us
    ppermute x5, starting transfers between devices, local(): lax.ppermute(parts[0] if len(parts) == 1 else jnp.concatenate(parts), axi...  6.61 us
    ppermute x1, starting transfers between devices, local(): rows = lax.ppermute(rotation, ('dom', 'st'), shift)  5.18 us
    ppermute x1, starting transfers between devices, local(): high = lax.ppermute(low_send, 'dom', down)  3.64 us
    pallas_call x1, Pallas kernels, prepare(): pl.pallas_call(prepare_kernel, grid=(planes // group,), in_specs=[pl.Bloc...  3.02 us
  transfers between devices with their start and end apart: 9, of which 6 were waited for; matrix products, arithmetic and copies ran while one was open for 0% of the time, Pallas kernels for 17%

profile of v6, /device:TPU:2, one launch (start us, length us, event | category | flops | bytes accessed | tf_op | source)
XLA Modules:
  0.0 88.5 jit_solution(7106484346973373607)
XLA Ops:
  0.0 0.0 copy-start
  0.0 0.0 copy-start.1
  0.0 1.4 %edges.1 = (bf16[72,1024]{1,0:T(8,128)(2,1)S(1)}, bf16[72,1024]{1,0:T(8,128)(2,1)S(1)}) custom-call(bf16[16,64,1024]{2,1,0:T(8,128)(2,1)} %last_ref.1, bf16[16,64,1024]{2,1,0:T(8,128)(2,1)} %last_ref.1, bf16[64,1024]{1,0:T(8,128)(2,1)} %pot_last_ref.1, bf16[64,1024]{1,0:T(8,128)(2,1)} %pot_last_ref.1), custom_call_target="tpu_custom_call" | custom-call | tf_op jit(solution)/shard_map/edges/pallas_call | solution.py:72
  1.4 1.9 %collective-permute-start.1 = (bf16[72,1024]{1,0:T(8,128)(2,1)S(1)}, bf16[72,1024]{1,0:T(8,128)(2,1)S(1)}, u32[]{:S(2)}, u32[]{:S(2)}) collective-permute-start(bf16[72,1024]{1,0:T(8,128)(2,1)S(1)} %get-tuple-element.17), channel_id=1, source_target_pairs={{0,32},{32,64},{64,96},{96,128},{128,160},{160,192},{192,224},{1,3... | collective-permute-start | bytes 442376 | tf_op jit(solution)/shard_map/ppermute | solution.py:415
  3.3 0.0 copy-start.2
  3.4 3.6 %collective-permute-start.2 = (bf16[72,1024]{1,0:T(8,128)(2,1)S(1)}, bf16[72,1024]{1,0:T(8,128)(2,1)S(1)}, u32[]{:S(2)}, u32[]{:S(2)}) collective-permute-start(bf16[72,1024]{1,0:T(8,128)(2,1)S(1)} %get-tuple-element.18), channel_id=1, source_target_pairs={{32,0},{64,32},{96,64},{128,96},{160,128},{192,160},{224,192},{33,... | collective-permute-start | bytes 442376 | tf_op jit(solution)/shard_map/ppermute | solution.py:416
  7.0 0.0 copy-done
  7.0 0.0 copy-done.1
  7.0 3.0 %prepare.1 = (bf16[64,128,128]{2,1,0:T(8,128)(2,1)S(1)}, f32[64,128,128]{2,1,0:T(8,128)S(1)}) custom-call(bf16[16,64,1024]{2,1,0:T(8,128)(2,1)S(1)} %copy-done, bf16[64,1024]{1,0:T(8,128)(2,1)S(1)} %copy-done.1), custom_call_target="tpu_custom_call" | custom-call | flops 2147483648 | bytes 8388608 | tf_op jit(solution)/shard_map/prepare/pallas_call | solution.py:127
  10.1 0.0 copy-done.2
  10.1 5.2 %collective-permute-start = (bf16[16,512]{1,0:T(8,128)(2,1)S(1)}, bf16[16,512]{1,0:T(8,128)(2,1)S(1)}, u32[]{:S(2)}, u32[]{:S(2)}) collective-permute-start(bf16[16,512]{1,0:T(8,128)(2,1)S(1)} %copy-done.2), channel_id=1, source_target_pairs={{0,0},{1,1},{2,2},{3,3},{4,4},{5,5},{6,6},{7,7},{8,8},{9,9},{10,10... | collective-permute-start | bytes 49160 | tf_op jit(solution)/shard_map/ppermute | solution.py:425
  15.3 0.0 collective-permute-done.1.low_ref
  15.3 0.0 collective-permute-done.2.high_ref
  15.3 11.0 %chebyshev.1 = bf16[32,16,2048]{2,1,0:T(8,128)(2,1)} custom-call(bf16[64,128,128]{2,1,0:T(8,128)(2,1)S(1)} %get-tuple-element.15.field_ref, f32[64,128,128]{2,1,0:T(8,128)S(1)} %get-tuple-element.16.pot_ref, bf16[72,1024]{1,0:T(8,128)(2,1)S(1)} %collective-permute-done.1.low_ref, bf16[72,1024]{1,0:T(8,128)(2,1)S(1)} %collective-permute-done.2.high_ref), custom_call_target="tpu_custom_call" | custom-call | tf_op jit(solution)/shard_map/chebyshev/pallas_call | solution.py:310
  26.3 0.0 collective-permute-done.refs_0_
  26.3 9.7 %all-to-all-start = ((bf16[32,16,2048]{2,1,0:T(8,128)(2,1)}), bf16[32,16,2048]{2,1,0:T(8,128)(2,1)S(1)}, u32[]{:S(2)}, u32[]{:S(2)}) async-start(bf16[32,16,2048]{2,1,0:T(8,128)(2,1)} %chebyshev.1), calls=%async_computation | async-start | bytes 4194304 | tf_op jit(solution)/shard_map/all_to_all | solution.py:428
  36.0 1.9 %collective-permute-start.3 = (bf16[16,512]{1,0:T(8,128)(2,1)S(1)}, bf16[16,512]{1,0:T(8,128)(2,1)S(1)}, u32[]{:S(2)}, u32[]{:S(2)}) collective-permute-start(bf16[16,512]{1,0:T(8,128)(2,1)S(1)} %collective-permute-done.refs_0_), channel_id=1, source_target_pairs={{0,8},{1,9},{2,10},{3,11},{4,12},{5,13},{6,14},{7,15},{8,16},{9,17... | collective-permute-start | bytes 49160 | tf_op jit(solution)/shard_map/ppermute | solution.py:438
  37.9 4.2 %collective-permute-done.3.refs_1_ = bf16[16,512]{1,0:T(8,128)(2,1)S(1)} collective-permute-done((bf16[16,512]{1,0:T(8,128)(2,1)S(1)}, bf16[16,512]{1,0:T(8,128)(2,1)S(1)}, u32[]{:S(2)}, u32[]{:S(2)}) %collective-permute-start.3) | collective-permute-done | bytes 16416 | tf_op jit(solution)/shard_map/ppermute | solution.py:438
  42.1 1.8 %collective-permute-start.4 = (bf16[32,512]{1,0:T(8,128)(2,1)S(1)}, bf16[32,512]{1,0:T(8,128)(2,1)S(1)}, u32[]{:S(2)}, u32[]{:S(2)}) collective-permute-start(bf16[32,512]{1,0:T(8,128)(2,1)S(1)} %pad_maximum_fusion.2), channel_id=1, source_target_pairs={{0,16},{1,17},{2,18},{3,19},{4,20},{5,21},{6,22},{7,23},{8,24},{9,... | collective-permute-start | bytes 98312 | tf_op jit(solution)/shard_map/ppermute | solution.py:438
  43.9 4.2 %collective-permute-done.4.refs_2_ = bf16[32,512]{1,0:T(8,128)(2,1)S(1)} collective-permute-done((bf16[32,512]{1,0:T(8,128)(2,1)S(1)}, bf16[32,512]{1,0:T(8,128)(2,1)S(1)}, u32[]{:S(2)}, u32[]{:S(2)}) %collective-permute-start.4) | collective-permute-done | bytes 32800 | tf_op jit(solution)/shard_map/ppermute | solution.py:438
  48.1 0.0 collective-permute-start.5
  48.1 1.2 %collective-permute-done.5.refs_3_ = bf16[64,512]{1,0:T(8,128)(2,1)S(1)} collective-permute-done((bf16[64,512]{1,0:T(8,128)(2,1)S(1)}, bf16[64,512]{1,0:T(8,128)(2,1)S(1)}, u32[]{:S(2)}, u32[]{:S(2)}) %collective-permute-start.5) | collective-permute-done | bytes 65568 | tf_op jit(solution)/shard_map/ppermute | solution.py:438
  49.4 1.6 %collective-permute-start.6 = (bf16[128,512]{1,0:T(8,128)(2,1)S(1)}, bf16[128,512]{1,0:T(8,128)(2,1)S(1)}, u32[]{:S(2)}, u32[]{:S(2)}) collective-permute-start(bf16[128,512]{1,0:T(8,128)(2,1)S(1)} %pad_maximum_fusion), channel_id=1, source_target_pairs={{0,64},{32,96},{64,128},{96,160},{128,192},{160,224},{192,0},{224,... | collective-permute-start | bytes 393224 | tf_op jit(solution)/shard_map/ppermute | solution.py:438
  51.0 4.0 %collective-permute-done.6.refs_4_ = bf16[128,512]{1,0:T(8,128)(2,1)S(1)} collective-permute-done((bf16[128,512]{1,0:T(8,128)(2,1)S(1)}, bf16[128,512]{1,0:T(8,128)(2,1)S(1)}, u32[]{:S(2)}, u32[]{:S(2)}) %collective-permute-start.6) | collective-permute-done | bytes 131104 | tf_op jit(solution)/shard_map/ppermute | solution.py:438
  55.0 1.3 %collective-permute-start.7 = (bf16[256,512]{1,0:T(8,128)(2,1)S(1)}, bf16[256,512]{1,0:T(8,128)(2,1)S(1)}, u32[]{:S(2)}, u32[]{:S(2)}) collective-permute-start(bf16[256,512]{1,0:T(8,128)(2,1)S(1)} %constant_dynamic-update-slice_fusion), channel_id=1, source_target_pairs={{0,128},{32,160},{64,192},{96,224},{128,0},{160,32},{192,64},{224,... | collective-permute-start | bytes 786440 | tf_op jit(solution)/shard_map/ppermute | solution.py:438
  56.4 0.1 stack.15.place_ref
  56.5 7.7 %collective-permute-done.7.refs_5_ = bf16[256,512]{1,0:T(8,128)(2,1)S(1)} collective-permute-done((bf16[256,512]{1,0:T(8,128)(2,1)S(1)}, bf16[256,512]{1,0:T(8,128)(2,1)S(1)}, u32[]{:S(2)}, u32[]{:S(2)}) %collective-permute-start.7) | collective-permute-done | bytes 262176 | tf_op jit(solution)/shard_map/ppermute | solution.py:438
  64.1 1.0 %order.1.r_ref = bf16[512,512]{1,0:T(8,128)(2,1)S(1)} custom-call(s32[5]{0:T(128)S(1)} %stack.15.place_ref, bf16[16,512]{1,0:T(8,128)(2,1)S(1)} %collective-permute-done.refs_0_, bf16[16,512]{1,0:T(8,128)(2,1)S(1)} %collective-permute-done.3.refs_1_, bf16[32,512]{1,0:T(8,128)(2,1)S(1)} %collective-permute-done.4.refs_2_, ...), custom_call_target="tpu_custom_call" | custom-call | tf_op jit(solution)/shard_map/order/pallas_call | solution.py:393
  65.1 21.2 %all-to-all-done = bf16[32,16,2048]{2,1,0:T(8,128)(2,1)S(1)} async-done(((bf16[32,16,2048]{2,1,0:T(8,128)(2,1)}), bf16[32,16,2048]{2,1,0:T(8,128)(2,1)S(1)}, u32[]{:S(2)}, u32[]{:S(2)}) %all-to-all-start) | async-done | bytes 2097184 | tf_op jit(solution)/shard_map/all_to_all | solution.py:428
  86.3 2.2 %rotate.1 = bf16[512,2048]{1,0:T(8,128)(2,1)} custom-call(bf16[512,512]{1,0:T(8,128)(2,1)S(1)} %order.1.r_ref, bf16[512,2048]{1,0:T(8,128)(2,1)S(1)} %bitcast.4), custom_call_target="tpu_custom_call" | custom-call | tf_op jit(solution)/shard_map/rotate/pallas_call | solution.py:354
  (8 shorter events, 0.0 us)
Async XLA Ops:
  0.0 7.0 %copy-start = (bf16[16,64,1024]{2,1,0:T(8,128)(2,1)S(1)}, bf16[16,64,1024]{2,1,0:T(8,128)(2,1)}, u32[]{:S(2)}) copy-start(bf16[16,64,1024]{2,1,0:T(8,128)(2,1)} %last_ref.1) | copy-start | bytes 6291460
  0.0 7.0 %copy-start.1 = (bf16[64,1024]{1,0:T(8,128)(2,1)S(1)}, bf16[64,1024]{1,0:T(8,128)(2,1)}, u32[]{:S(2)}) copy-start(bf16[64,1024]{1,0:T(8,128)(2,1)} %pot_last_ref.1) | copy-start | bytes 393220
  1.4 13.8 %collective-permute-start.1 = (bf16[72,1024]{1,0:T(8,128)(2,1)S(1)}, bf16[72,1024]{1,0:T(8,128)(2,1)S(1)}, u32[]{:S(2)}, u32[]{:S(2)}) collective-permute-start(bf16[72,1024]{1,0:T(8,128)(2,1)S(1)} %get-tuple-element.17), channel_id=1, source_target_pairs={{0,32},{32,64},{64,96},{96,128},{128,160},{160,192},{192,224},{1,3... | collective-permute-start | bytes 442376 | tf_op jit(solution)/shard_map/ppermute | solution.py:415
  3.3 6.7 %copy-start.2 = (bf16[16,512]{1,0:T(8,128)(2,1)S(1)}, bf16[16,512]{1,0:T(8,128)(2,1)}, u32[]{:S(2)}) copy-start(bf16[16,512]{1,0:T(8,128)(2,1)} %param.5) | copy-start | bytes 49156
  3.4 11.9 %collective-permute-start.2 = (bf16[72,1024]{1,0:T(8,128)(2,1)S(1)}, bf16[72,1024]{1,0:T(8,128)(2,1)S(1)}, u32[]{:S(2)}, u32[]{:S(2)}) collective-permute-start(bf16[72,1024]{1,0:T(8,128)(2,1)S(1)} %get-tuple-element.18), channel_id=1, source_target_pairs={{32,0},{64,32},{96,64},{128,96},{160,128},{192,160},{224,192},{33,... | collective-permute-start | bytes 442376 | tf_op jit(solution)/shard_map/ppermute | solution.py:416
  10.1 16.3 %collective-permute-start = (bf16[16,512]{1,0:T(8,128)(2,1)S(1)}, bf16[16,512]{1,0:T(8,128)(2,1)S(1)}, u32[]{:S(2)}, u32[]{:S(2)}) collective-permute-start(bf16[16,512]{1,0:T(8,128)(2,1)S(1)} %copy-done.2), channel_id=1, source_target_pairs={{0,0},{1,1},{2,2},{3,3},{4,4},{5,5},{6,6},{7,7},{8,8},{9,9},{10,10... | collective-permute-start | bytes 49160 | tf_op jit(solution)/shard_map/ppermute | solution.py:425
  26.3 60.0 %all-to-all-start = ((bf16[32,16,2048]{2,1,0:T(8,128)(2,1)}), bf16[32,16,2048]{2,1,0:T(8,128)(2,1)S(1)}, u32[]{:S(2)}, u32[]{:S(2)}) async-start(bf16[32,16,2048]{2,1,0:T(8,128)(2,1)} %chebyshev.1), calls=%async_computation | async-start | bytes 4194304 | tf_op jit(solution)/shard_map/all_to_all | solution.py:428
  36.0 6.1 %collective-permute-start.3 = (bf16[16,512]{1,0:T(8,128)(2,1)S(1)}, bf16[16,512]{1,0:T(8,128)(2,1)S(1)}, u32[]{:S(2)}, u32[]{:S(2)}) collective-permute-start(bf16[16,512]{1,0:T(8,128)(2,1)S(1)} %collective-permute-done.refs_0_), channel_id=1, source_target_pairs={{0,8},{1,9},{2,10},{3,11},{4,12},{5,13},{6,14},{7,15},{8,16},{9,17... | collective-permute-start | bytes 49160 | tf_op jit(solution)/shard_map/ppermute | solution.py:438
  42.1 6.0 %collective-permute-start.4 = (bf16[32,512]{1,0:T(8,128)(2,1)S(1)}, bf16[32,512]{1,0:T(8,128)(2,1)S(1)}, u32[]{:S(2)}, u32[]{:S(2)}) collective-permute-start(bf16[32,512]{1,0:T(8,128)(2,1)S(1)} %pad_maximum_fusion.2), channel_id=1, source_target_pairs={{0,16},{1,17},{2,18},{3,19},{4,20},{5,21},{6,22},{7,23},{8,24},{9,... | collective-permute-start | bytes 98312 | tf_op jit(solution)/shard_map/ppermute | solution.py:438
  48.1 1.3 %collective-permute-start.5 = (bf16[64,512]{1,0:T(8,128)(2,1)S(1)}, bf16[64,512]{1,0:T(8,128)(2,1)S(1)}, u32[]{:S(2)}, u32[]{:S(2)}) collective-permute-start(bf16[64,512]{1,0:T(8,128)(2,1)S(1)} %pad_maximum_fusion.1), channel_id=1, source_target_pairs={{0,32},{32,0},{64,96},{96,64},{128,160},{160,128},{192,224},{224,1... | collective-permute-start | bytes 196616 | tf_op jit(solution)/shard_map/ppermute | solution.py:438
  49.4 5.6 %collective-permute-start.6 = (bf16[128,512]{1,0:T(8,128)(2,1)S(1)}, bf16[128,512]{1,0:T(8,128)(2,1)S(1)}, u32[]{:S(2)}, u32[]{:S(2)}) collective-permute-start(bf16[128,512]{1,0:T(8,128)(2,1)S(1)} %pad_maximum_fusion), channel_id=1, source_target_pairs={{0,64},{32,96},{64,128},{96,160},{128,192},{160,224},{192,0},{224,... | collective-permute-start | bytes 393224 | tf_op jit(solution)/shard_map/ppermute | solution.py:438
  55.0 9.1 %collective-permute-start.7 = (bf16[256,512]{1,0:T(8,128)(2,1)S(1)}, bf16[256,512]{1,0:T(8,128)(2,1)S(1)}, u32[]{:S(2)}, u32[]{:S(2)}) collective-permute-start(bf16[256,512]{1,0:T(8,128)(2,1)S(1)} %constant_dynamic-update-slice_fusion), channel_id=1, source_target_pairs={{0,128},{32,160},{64,192},{96,224},{128,0},{160,32},{192,64},{224,... | collective-permute-start | bytes 786440 | tf_op jit(solution)/shard_map/ppermute | solution.py:438
